TPU v7x, 32 devices: a whole 2x2x4 slice. The times are simulated.
32 devices in a mesh: gx: 4 (over y, x), gy: 4 (over z), gz: 2 (over core).
Axes of the slice: x: 2, y: 2, z: 4, core: 2. Of those that a mesh axis runs over, the one named last changes fastest.
Arguments:
- viscosity: float32 [32, 64, 512], P('gz', 'gy', 'gx'), may hold values from 0.1 to 10
- adjoint_source: float32 [32, 64, 512], P('gz', 'gy', 'gx'), may hold values from -6 to 6
- forward_velocity: float32 [32, 64, 512], P('gz', 'gy', 'gx'), may hold values from -6 to 6
- friction: float32 [64, 512], P('gy', 'gx'), may hold values from 0.1 to 10
- ice_mask: int32 [64, 512], P('gy', 'gx'), may hold values 0 or 1
- grounded_mask: int32 [64, 512], P('gy', 'gx'), may hold values 0 or 1
Outputs:
- adjoint: float32 [32, 64, 512], P('gz', 'gy', 'gx')
- gradient: float32 [64, 512], P('gy', ('gx', 'gz'))
All inputs are finite; a program needn't handle non-finite values. No bound on the sum of `ice_mask` or of `grounded_mask` on one device may be relied on, other than what follows from the above.
Results may differ from a plain program's by a relative error of at most 0.00002.
Values sent between devices are 32-bit elements; how exact they have to be, the bound alone decides.
No kernel may reach another device: no remote copies, remote signals or barrier semaphores. Data moves between devices by JAX's collectives and lax.ppermute only.
A program may use at most 64 MiB of HBM per device.

v0:
```python
import jax
import jax.numpy as jnp
from jax import lax
from jax.sharding import PartitionSpec as P

S0 = 4
S1 = 4
S2 = 8


OMEGA = 0.8
VERT = 4.0
HI = lax.Precision.HIGHEST
FINE_HALO = 12
MID_HALO = 6
POST_HALO = 4


def layer_halos(u):
    count = lax.axis_size("gz")
    head = u[:1]
    tail = u[-1:]
    if count == 2:
        first = lax.axis_index("gz") == 0
        got = lax.ppermute(jnp.where(first, tail, head), "gz", [(0, 1), (1, 0)])
        zero = jnp.zeros_like(got)
        return jnp.where(first, zero, got), jnp.where(first, got, zero)
    lo = lax.ppermute(tail, "gz", [(i, i + 1) for i in range(count - 1)])
    hi = lax.ppermute(head, "gz", [(i + 1, i) for i in range(count - 1)])
    return lo, hi


def extend_rows(a, h):
    count = lax.axis_size("gy")
    lo = lax.ppermute(a[:, -h:], "gy", [(i, i + 1) for i in range(count - 1)])
    hi = lax.ppermute(a[:, :h], "gy", [(i + 1, i) for i in range(count - 1)])
    return jnp.concatenate([lo, a, hi], axis=1)


def gather_blocks(a, axis):
    count = lax.axis_size(axis)
    got = [a]
    for s in range(1, count):
        got.append(lax.ppermute(a, axis, [(i, (i + s) % count) for i in range(count)]))
    rev = jnp.stack(got[::-1], axis=0)
    return jnp.roll(rev, lax.axis_index(axis) + 1, axis=0)


def crop(a, h_from, h_to):
    cut = h_from - h_to
    return a[:, cut : a.shape[1] - cut]


def row_mask(own_rows, h):
    g = lax.axis_index("gy") * own_rows - h + lax.broadcasted_iota(jnp.int32, (1, own_rows + 2 * h, 1), 1)
    return (g >= 0) & (g < own_rows * lax.axis_size("gy"))


def neighbours(u):
    zlo, zhi = layer_halos(u)
    zero_row = jnp.zeros_like(u[:, :1])
    zero_col = jnp.zeros_like(u[:, :, :1])
    zm = jnp.concatenate([zlo, u[:-1]], axis=0)
    zp = jnp.concatenate([u[1:], zhi], axis=0)
    ym = jnp.concatenate([zero_row, u[:, :-1]], axis=1)
    yp = jnp.concatenate([u[:, 1:], zero_row], axis=1)
    xm = jnp.concatenate([zero_col, u[:, :, :-1]], axis=2)
    xp = jnp.concatenate([u[:, :, 1:], zero_col], axis=2)
    return zm, zp, ym, yp, xm, xp


def face_set(eta):
    zm, zp, ym, yp, xm, xp = neighbours(eta)
    zlo = VERT * (0.5 * (eta + zm))
    zhi = VERT * (0.5 * (eta + zp))
    ylo = 0.5 * (eta + ym)
    yhi = 0.5 * (eta + yp)
    xlo = 0.5 * (eta + xm)
    xhi = 0.5 * (eta + xp)
    return (zlo, zhi, ylo, yhi, xlo, xhi)


def operate(u, coef):
    zlo, zhi, ylo, yhi, xlo, xhi, extra = coef
    zm, zp, ym, yp, xm, xp = neighbours(u)
    out = zlo * (u - zm) + zhi * (u - zp)
    out = out + ylo * (u - ym) + yhi * (u - yp)
    out = out + xlo * (u - xm) + xhi * (u - xp)
    return out + extra * u


def diagonal(coef):
    zlo, zhi, ylo, yhi, xlo, xhi, extra = coef
    return zlo + zhi + ylo + yhi + xlo + xhi + extra


def pick(n, parity):
    src = lax.broadcasted_iota(jnp.int32, (n, n // 2), 0)
    dst = lax.broadcasted_iota(jnp.int32, (n, n // 2), 1)
    return (src == 2 * dst + parity).astype(jnp.float32)


def cols(a, parity):
    return jnp.dot(a, pick(a.shape[-1], parity), precision=HI)


def rows(a, parity):
    return jnp.einsum("yr,zyx->zrx", pick(a.shape[1], parity), a, precision=HI)


def mean_four(a):
    r0 = rows(a, 0)
    r1 = rows(a, 1)
    return 0.25 * (cols(r0, 0) + cols(r1, 0) + cols(r0, 1) + cols(r1, 1))


def coarsen(coef):
    zlo, zhi, ylo, yhi, xlo, xhi, extra = coef
    cxlo = 0.125 * cols(rows(xlo, 0) + rows(xlo, 1), 0)
    cxhi = 0.125 * cols(rows(xhi, 0) + rows(xhi, 1), 1)
    ylo0 = rows(ylo, 0)
    yhi1 = rows(yhi, 1)
    cylo = 0.125 * (cols(ylo0, 0) + cols(ylo0, 1))
    cyhi = 0.125 * (cols(yhi1, 0) + cols(yhi1, 1))
    return (mean_four(zlo), mean_four(zhi), cylo, cyhi, cxlo, cxhi, mean_four(extra))


def spread(n):
    src = lax.broadcasted_iota(jnp.int32, (n, 2 * n), 0)
    dst = lax.broadcasted_iota(jnp.int32, (n, 2 * n), 1)
    return (src == dst // 2).astype(jnp.float32)


def prolong(field):
    wide = jnp.dot(field, spread(field.shape[-1]), precision=HI)
    return jnp.einsum("ry,zrx->zyx", spread(field.shape[1]), wide, precision=HI)


def sweep(field, rhs, coef, diag, inside):
    new = field + OMEGA * (rhs - operate(field, coef)) / diag
    return jnp.where(inside, new, 0.0)


def smooth(field, rhs, coef, diag, inside, count):
    for i in range(count):
        field = sweep(field, rhs, coef, diag, inside)
    return field


def crop_all(arrs, h_from, h_to):
    return tuple(crop(a, h_from, h_to) for a in arrs)


def body_wide(viscosity, adjoint_source, forward_velocity, friction, ice_mask, grounded_mask):
    layers = viscosity.shape[0]
    own_rows = viscosity.shape[1]
    mid_rows = own_rows // 2
    cols_own = viscosity.shape[2]
    half_cols = cols_own // 2
    gz = lax.axis_index("gz")
    gy = lax.axis_index("gy")
    total_layers = layers * lax.axis_size("gz")
    layer = (gz * layers + jnp.arange(layers)).astype(jnp.float32)
    profile = (jnp.float32(total_layers) - layer) / jnp.float32(total_layers)
    wsq = profile * profile
    icef = ice_mask.astype(jnp.float32)
    groundf = grounded_mask.astype(jnp.float32)
    base = 0.05 + 2.0 * (1.0 - icef)
    ground_fric = groundf * friction
    stacked = jnp.concatenate([viscosity, adjoint_source, base[None], ground_fric[None]], axis=0)
    gathered = gather_blocks(stacked, "gx")
    gathered = jnp.concatenate([gathered[i] for i in range(gathered.shape[0])], axis=2)
    hv = FINE_HALO + 1
    ext = extend_rows(gathered, hv)
    visc_e = ext[:layers]
    src_e = crop(ext[layers : 2 * layers], hv, FINE_HALO)
    base_e = crop(ext[2 * layers : 2 * layers + 1], hv, FINE_HALO)[0]
    gfr_e = crop(ext[2 * layers + 1 : 2 * layers + 2], hv, FINE_HALO)[0]
    extra = base_e[None, :, :] + gfr_e[None, :, :] * wsq[:, None, None]
    fine = crop_all(face_set(visc_e), hv, FINE_HALO) + (extra,)
    dfine = diagonal(fine)
    middle = coarsen(fine)
    dmid = diagonal(middle)
    coarse_own = coarsen(crop_all(middle, FINE_HALO // 2, 0))
    coarse_all = gather_blocks(jnp.concatenate(coarse_own, axis=0), "gy")
    coarse_all = jnp.concatenate([coarse_all[i] for i in range(coarse_all.shape[0])], axis=1)
    coarse = tuple(coarse_all[i * layers : (i + 1) * layers] for i in range(7))
    dcoarse = diagonal(coarse)
    in_fine = row_mask(own_rows, FINE_HALO)
    in_mid = row_mask(mid_rows, FINE_HALO // 2)

    lam = jnp.where(in_fine, OMEGA * src_e / dfine, 0.0)
    lam = smooth(lam, src_e, fine, dfine, in_fine, S0 - 1)
    b_mid = mean_four(src_e - operate(lam, fine))
    e_mid = jnp.where(in_mid, OMEGA * b_mid / dmid, 0.0)
    e_mid = smooth(e_mid, b_mid, middle, dmid, in_mid, S1 - 1)
    hm = FINE_HALO // 2
    res_mid = crop(b_mid - operate(e_mid, middle), hm, 0)
    b_low = gather_blocks(mean_four(res_mid), "gy")
    b_low = jnp.concatenate([b_low[i] for i in range(b_low.shape[0])], axis=1)
    e_low = OMEGA * b_low / dcoarse
    ones = jnp.ones((1, b_low.shape[1], 1), dtype=bool)
    e_low = smooth(e_low, b_low, coarse, dcoarse, ones, S2 - 1)

    pair = jnp.concatenate([crop(e_mid, hm, 0), crop(b_mid, hm, 0)], axis=0)
    pair = extend_rows(pair, MID_HALO)
    e_mid = pair[:layers]
    b_mid = pair[layers:]
    low_rows = own_rows // 4
    ch = MID_HALO // 2
    padded = jnp.pad(e_low, ((0, 0), (ch, ch), (0, 0)))
    e_near = lax.dynamic_slice_in_dim(padded, gy * low_rows, low_rows + 2 * ch, 1)
    e_mid = e_mid + prolong(e_near)
    middle_p = crop_all(middle, hm, MID_HALO)
    dmid_p = crop(dmid, hm, MID_HALO)
    in_mid_p = row_mask(mid_rows, MID_HALO)
    e_mid = smooth(e_mid, b_mid, middle_p, dmid_p, in_mid_p, S1)

    lam = crop(lam, FINE_HALO, POST_HALO) + prolong(crop(e_mid, MID_HALO, POST_HALO // 2))
    fine_p = crop_all(fine, FINE_HALO, POST_HALO)
    dfine_p = crop(dfine, FINE_HALO, POST_HALO)
    src_p = crop(src_e, FINE_HALO, POST_HALO)
    in_fine_p = row_mask(own_rows, POST_HALO)
    lam = smooth(lam, src_p, fine_p, dfine_p, in_fine_p, S0)
    lam = crop(lam, POST_HALO, 0)

    own = lax.dynamic_slice_in_dim(lam, lax.axis_index("gx") * cols_own, cols_own, 2)
    column = jnp.sum(wsq[:, None, None] * forward_velocity * own, axis=0)
    summed = lax.psum(column, "gz")
    terms = -ground_fric * summed
    gradient = lax.dynamic_slice_in_dim(terms, gz * half_cols, half_cols, 1)
    return (own, gradient)


def n_layer_halos(u):
    count = lax.axis_size("gz")
    head = u[:1]
    tail = u[-1:]
    if count == 2:
        first = lax.axis_index("gz") == 0
        got = lax.ppermute(jnp.where(first, tail, head), "gz", [(0, 1), (1, 0)])
        zero = jnp.zeros_like(got)
        return jnp.where(first, zero, got), jnp.where(first, got, zero)
    lo = lax.ppermute(tail, "gz", [(i, i + 1) for i in range(count - 1)])
    hi = lax.ppermute(head, "gz", [(i + 1, i) for i in range(count - 1)])
    return lo, hi


def n_row_halos(u):
    count = lax.axis_size("gy")
    lo = lax.ppermute(u[:, -1:], "gy", [(i, i + 1) for i in range(count - 1)])
    hi = lax.ppermute(u[:, :1], "gy", [(i + 1, i) for i in range(count - 1)])
    return lo, hi


def n_neighbours(u):
    zlo, zhi = n_layer_halos(u)
    ylo, yhi = n_row_halos(u)
    zero = jnp.zeros_like(u[:, :, :1])
    zm = jnp.concatenate([zlo, u[:-1]], axis=0)
    zp = jnp.concatenate([u[1:], zhi], axis=0)
    ym = jnp.concatenate([ylo, u[:, :-1]], axis=1)
    yp = jnp.concatenate([u[:, 1:], yhi], axis=1)
    xm = jnp.concatenate([zero, u[:, :, :-1]], axis=2)
    xp = jnp.concatenate([u[:, :, 1:], zero], axis=2)
    return zm, zp, ym, yp, xm, xp


def n_face_set(eta):
    zm, zp, ym, yp, xm, xp = n_neighbours(eta)
    zlo = VERT * (0.5 * (eta + zm))
    zhi = VERT * (0.5 * (eta + zp))
    ylo = 0.5 * (eta + ym)
    yhi = 0.5 * (eta + yp)
    xlo = 0.5 * (eta + xm)
    xhi = 0.5 * (eta + xp)
    return (zlo, zhi, ylo, yhi, xlo, xhi)


def n_operate(u, coef):
    zlo, zhi, ylo, yhi, xlo, xhi, extra = coef
    zm, zp, ym, yp, xm, xp = n_neighbours(u)
    out = zlo * (u - zm) + zhi * (u - zp)
    out = out + ylo * (u - ym) + yhi * (u - yp)
    out = out + xlo * (u - xm) + xhi * (u - xp)
    return out + extra * u


def n_diagonal(coef):
    zlo, zhi, ylo, yhi, xlo, xhi, extra = coef
    return zlo + zhi + ylo + yhi + xlo + xhi + extra


def n_pick_matrix(cols):
    half = cols // 2
    src = lax.broadcasted_iota(jnp.int32, (cols, cols), 0)
    dst = lax.broadcasted_iota(jnp.int32, (cols, cols), 1)
    want = jnp.where(dst < half, 2 * dst, 2 * (dst - half) + 1)
    return (src == want).astype(jnp.float32)


def n_split_x(a):
    cols = a.shape[-1]
    both = jnp.dot(a, n_pick_matrix(cols), precision=HI)
    return both[..., : cols // 2], both[..., cols // 2 :]


def n_mean_four(a):
    e0, o0 = n_split_x(a[:, 0::2])
    e1, o1 = n_split_x(a[:, 1::2])
    return 0.25 * (e0 + e1 + o0 + o1)


def n_coarsen(coef):
    zlo, zhi, ylo, yhi, xlo, xhi, extra = coef
    xlo_e, _ = n_split_x(xlo[:, 0::2] + xlo[:, 1::2])
    _, xhi_o = n_split_x(xhi[:, 0::2] + xhi[:, 1::2])
    ylo_e, ylo_o = n_split_x(ylo[:, 0::2])
    yhi_e, yhi_o = n_split_x(yhi[:, 1::2])
    cxlo = 0.125 * xlo_e
    cxhi = 0.125 * xhi_o
    cylo = 0.125 * (ylo_e + ylo_o)
    cyhi = 0.125 * (yhi_e + yhi_o)
    return (n_mean_four(zlo), n_mean_four(zhi), cylo, cyhi, cxlo, cxhi, n_mean_four(extra))


def n_prolong(field):
    cols = field.shape[-1]
    src = lax.broadcasted_iota(jnp.int32, (cols, 2 * cols), 0)
    dst = lax.broadcasted_iota(jnp.int32, (cols, 2 * cols), 1)
    spread = (src == dst // 2).astype(jnp.float32)
    wide = jnp.dot(field, spread, precision=HI)
    return jnp.repeat(wide, 2, axis=1)


def n_sweep(field, rhs, coef, diag):
    return field + OMEGA * (rhs - n_operate(field, coef)) / diag


def n_body(viscosity, adjoint_source, forward_velocity, friction, ice_mask, grounded_mask):
    layers = viscosity.shape[0]
    cols = viscosity.shape[2]
    half_cols = cols // 2
    gz = lax.axis_index("gz")
    total_layers = layers * lax.axis_size("gz")
    layer = (gz * layers + jnp.arange(layers)).astype(jnp.float32)
    profile = (jnp.float32(total_layers) - layer) / jnp.float32(total_layers)
    wsq = profile * profile
    icef = ice_mask.astype(jnp.float32)
    groundf = grounded_mask.astype(jnp.float32)
    base = 0.05 + 2.0 * (1.0 - icef)
    ground_fric = groundf * friction
    stacked = jnp.concatenate([viscosity, adjoint_source, base[None], ground_fric[None]], axis=0)
    gathered = lax.all_gather(stacked, "gx", axis=0, tiled=False)
    count_x = gathered.shape[0]
    gathered = jnp.concatenate([gathered[i] for i in range(count_x)], axis=2)
    visc_all = gathered[:layers]
    source_all = gathered[layers : 2 * layers]
    base_all = gathered[2 * layers]
    gfr_all = gathered[2 * layers + 1]
    extra = base_all[None, :, :] + gfr_all[None, :, :] * wsq[:, None, None]
    fine = n_face_set(visc_all) + (extra,)
    dfine = n_diagonal(fine)
    middle = n_coarsen(fine)
    dmid = n_diagonal(middle)
    coarse = n_coarsen(middle)
    dcoarse = n_diagonal(coarse)
    lam = OMEGA * source_all / dfine
    for i in range(S0 - 1):
        lam = n_sweep(lam, source_all, fine, dfine)
    b_mid = n_mean_four(source_all - n_operate(lam, fine))
    e_mid = OMEGA * b_mid / dmid
    for i in range(S1 - 1):
        e_mid = n_sweep(e_mid, b_mid, middle, dmid)
    b_low = n_mean_four(b_mid - n_operate(e_mid, middle))
    e_low = OMEGA * b_low / dcoarse
    for i in range(S2 - 1):
        e_low = n_sweep(e_low, b_low, coarse, dcoarse)
    e_mid = e_mid + n_prolong(e_low)
    for i in range(S1):
        e_mid = n_sweep(e_mid, b_mid, middle, dmid)
    lam = lam + n_prolong(e_mid)
    for i in range(S0):
        lam = n_sweep(lam, source_all, fine, dfine)
    own = lax.dynamic_slice_in_dim(lam, lax.axis_index("gx") * cols, cols, 2)
    column = jnp.sum(wsq[:, None, None] * forward_velocity * own, axis=0)
    summed = lax.psum(column, "gz")
    terms = -ground_fric * summed
    gradient = lax.dynamic_slice_in_dim(terms, gz * half_cols, half_cols, 1)
    return (own, gradient)


def body(viscosity, *rest):
    layers, own_rows, cols_own = viscosity.shape
    cols_all = cols_own * lax.axis_size("gx")
    wide_bytes = 4 * layers * (own_rows + 2 * FINE_HALO + 2) * cols_all
    if FINE_HALO + 1 <= own_rows and MID_HALO <= own_rows // 2 and 20 * wide_bytes <= 40 * 2**20 and lax.axis_size("gy") <= 8:
        return body_wide(viscosity, *rest)
    return n_body(viscosity, *rest)


def solution(mesh):
    placed = (
        P("gz", "gy", "gx"),
        P("gz", "gy", "gx"),
        P("gz", "gy", "gx"),
        P("gy", "gx"),
        P("gy", "gx"),
        P("gy", "gx"),
    )
    return jax.shard_map(
        body,
        mesh=mesh,
        in_specs=placed,
        out_specs=(P("gz", "gy", "gx"), P("gy", ("gx", "gz"))),
        check_vma=False,
    )
```

profile of v0, /device:TPU:0, one launch (start us, length us, event | category | flops | bytes accessed | tf_op | source)
XLA Modules:
  0.0 200.6 jit_solution(12718351764460151041)
XLA Ops:
  3.1 3.9 %collective-permute-start = (f32[34,16,128]{2,1,0:T(8,128)S(1)}, f32[34,16,128]{2,1,0:T(8,128)S(1)}, u32[]{:S(2)}, u32[]{:S(2)}) collective-permute-start(f32[34,16,128]{2,1,0:T(8,128)S(1)} %pad_maximum_fusion.4), channel_id=1, source_target_pairs={{0,24},{8,0},{16,8},{24,16},{1,25},{9,1},{17,9},{25,17},{2,26},{10... | collective-permute-start | bytes 835592 | tf_op jit(solution)/shard_map/ppermute | solution.py:44
  14.1 7.0 %collective-permute-done.1 = f32[34,16,128]{2,1,0:T(8,128)S(1)} collective-permute-done((f32[34,16,128]{2,1,0:T(8,128)S(1)}, f32[34,16,128]{2,1,0:T(8,128)S(1)}, u32[]{:S(2)}, u32[]{:S(2)}) %collective-permute-start.1) | collective-permute-done | bytes 278560 | tf_op jit(solution)/shard_map/ppermute | solution.py:44
  25.2 5.7 %collective-permute-start.3 = (f32[34,13,512]{2,0,1:T(8,128)}, f32[34,13,512]{2,0,1:T(8,128)}, u32[]{:S(2)}, u32[]{:S(2)}) collective-permute-start(f32[34,13,512]{2,0,1:T(8,128)} %copy.28), channel_id=1, source_target_pairs={{0,2},{2,4},{4,6},{1,3},{3,5},{5,7},{8,10},{10,12},{12,14},{9,11},... | collective-permute-start | bytes 2715656 | tf_op jit(solution)/shard_map/ppermute | solution.py:35
  35.0 12.4 %collective-permute-done.4 = f32[34,13,512]{2,0,1:T(8,128)S(1)} collective-permute-done((f32[34,13,512]{2,0,1:T(8,128)S(1)}, f32[34,13,512]{2,0,1:T(8,128)S(1)}, u32[]{:S(2)}, u32[]{:S(2)}) %collective-permute-start.4) | collective-permute-done | bytes 905248 | tf_op jit(solution)/shard_map/ppermute | solution.py:36
  48.0 2.5 %collective-permute-done.3 = f32[34,13,512]{2,0,1:T(8,128)} collective-permute-done((f32[34,13,512]{2,0,1:T(8,128)}, f32[34,13,512]{2,0,1:T(8,128)}, u32[]{:S(2)}, u32[]{:S(2)}) %collective-permute-start.3) | collective-permute-done | bytes 905248 | tf_op jit(solution)/shard_map/ppermute | solution.py:35
  52.7 1.9 fusion.556
  54.6 2.1 %fusion.557 = (f32[16,41,512]{2,1,0:T(8,128)}, f32[16,41,512]{2,1,0:T(8,128)}) fusion(f32[34,42,512]{2,1,0:T(8,128)S(1)} %pad_maximum_fusion), kind=kLoop, calls=%fused_computation.770 | loop fusion | bytes 5373952 | tf_op jit(solution)/shard_map/slice | solution.py:65
  56.7 2.3 %fusion.558 = (f32[16,42,511]{2,1,0:T(8,128)}, f32[16,42,511]{2,1,0:T(8,128)}) fusion(f32[34,42,512]{2,1,0:T(8,128)S(1)} %pad_maximum_fusion), kind=kLoop, calls=%fused_computation.771 | loop fusion | bytes 5494272 | tf_op jit(solution)/shard_map/slice | solution.py:67
  63.2 5.5 %fusion = (f32[16,42,512]{2,1,0:T(8,128)S(1)}, f32[16,42,512]{2,1,0:T(8,128)S(1)}, f32[16,42,512]{2,1,0:T(8,128)S(1)}, f32[16,42,512]{2,1,0:T(8,128)S(1)}, f32[1...) fusion(f32[15,42,512]{2,1,0:T(8,128)} %get-tuple-element.16, f32[1,42,512]{2,1,0:T(8,128)} %get-tuple-element.191, ...), kind=kLoop, calls=%fused_computation.2 | loop fusion | flops 4816896 | bytes 17820416 | tf_op jit(solution)/shard_map/mul | solution.py:74
  68.7 3.1 %divide_select_fusion = (f32[16,40,512]{2,1,0:T(8,128)S(1)}, f32[16,40,512]{2,1,0:T(8,128)S(1)}) fusion(f32[34,42,512]{2,1,0:T(8,128)S(1)} %pad_maximum_fusion, pred[40]{0:T(512)(128)(4,1)} %compare_and_fusion.4, f32[16]{0:T(128)} %copy-done.5, f32[40,512]{1,0:T(8,128)S(1)} %get-tuple-element.23, f32[40,512]{1,0:T(8,128)S(1)} %get-tuple-element.22, ...), kind=kLoop, calls=%fused_computation.62 | loop fusion | flops 3604480 | bytes 11960424 | tf_op jit(solution)/shard_map/jit(_where)/select_n | solution.py:192
  95.4 3.9 %fusion.52 = f32[16,40,512]{2,1,0:T(8,128)S(1)} fusion(f32[16,40,512]{2,1,0:T(8,128)S(1)} %get-tuple-element.9, f32[16,40,511]{2,1,0:T(8,128)S(1)} %get-tuple-element.57, f32[16,40,511]{2,1,0:T(8,128)S(1)} %get-tuple-element.56, f32[16,39,512]{2,1,0:T(8,128)S(1)} %get-tuple-element.55, f32[16,39,512]{2,1,0:T(8,128)S(1)} %get-tuple-element.54, ...), kind=kLoop, calls=%fused_computation.69 | loop fusion | flops 10158080 | bytes 19754088 | tf_op jit(solution)/shard_map/jit(_where)/select_n | solution.py:141
  101.4 4.0 %fusion.51 = f32[16,40,512]{2,1,0:T(8,128)S(1)} fusion(f32[16,40,512]{2,1,0:T(8,128)S(1)} %fusion.52, f32[16,40,512]{2,1,0:T(8,128)S(1)} %get-tuple-element.9, f32[16,40,511]{2,1,0:T(8,128)S(1)} %get-tuple-element.51, f32[16,40,511]{2,1,0:T(8,128)S(1)} %get-tuple-element.50, f32[16,39,512]{2,1,0:T(8,128)S(1)} %get-tuple-element.49, ...), kind=kLoop, calls=%fused_computation.68 | loop fusion | flops 9175040 | bytes 21064808 | tf_op jit(solution)/shard_map/jit(_where)/select_n | solution.py:141
  107.5 4.0 %fusion.50 = f32[16,40,512]{2,1,0:T(8,128)S(1)} fusion(f32[16,40,512]{2,1,0:T(8,128)S(1)} %fusion.51, f32[16,40,512]{2,1,0:T(8,128)S(1)} %get-tuple-element.9, f32[16,40,511]{2,1,0:T(8,128)S(1)} %get-tuple-element.45, f32[16,40,511]{2,1,0:T(8,128)S(1)} %get-tuple-element.44, f32[16,39,512]{2,1,0:T(8,128)S(1)} %get-tuple-element.43, ...), kind=kLoop, calls=%fused_computation.67 | loop fusion | flops 9175040 | bytes 21064808 | tf_op jit(solution)/shard_map/jit(_where)/select_n | solution.py:141
  113.7 3.6 %fusion.45 = (f32[16,40,512]{2,1,0:T(8,128)S(1)}, f32[16,40,512]{2,1,0:T(8,128)S(1)}) fusion(f32[16,40,512]{2,1,0:T(8,128)S(1)} %fusion.50, f32[15,40,512]{2,1,0:T(8,128)S(1)} %get-tuple-element.39, f32[1,40,512]{2,1,0:T(8,128)S(1)} %get-tuple-element.194, f32[1,40,512]{2,1,0:T(8,128)S(1)} %get-tuple-element.193, f32[15,40,512]{2,1,0:T(8,128)S(1)} %get-tuple-element.38, ...), kind=kLoop, calls=%fused_computation.59 | loop fusion | flops 7864320 | bytes 21064768 | tf_op jit(solution)/shard_map/sub | solution.py:194
  123.4 4.6 %collective-permute-start.19 = (f32[112,4,128]{2,0,1:T(8,128)S(1)}, f32[112,4,128]{2,0,1:T(8,128)S(1)}, u32[]{:S(2)}, u32[]{:S(2)}) collective-permute-start(f32[112,4,128]{2,0,1:T(8,128)S(1)} %fusion.63), channel_id=1, source_target_pairs={{0,6},{2,0},{4,2},{6,4},{1,7},{3,1},{5,3},{7,5},{8,14},{10,8},{12,... | collective-permute-start | bytes 688136 | tf_op jit(solution)/shard_map/ppermute | solution.py:44
  137.1 2.9 %collective-permute-start.16 = (f32[16,4,128]{2,0,1:T(8,128)S(1)}, f32[16,4,128]{2,0,1:T(8,128)S(1)}, u32[]{:S(2)}, u32[]{:S(2)}) collective-permute-start(f32[16,4,128]{2,0,1:T(8,128)S(1)} %fusion.74), channel_id=1, source_target_pairs={{0,6},{2,0},{4,2},{6,4},{1,7},{3,1},{5,3},{7,5},{8,14},{10,8},{12,... | collective-permute-start | bytes 98312 | tf_op jit(solution)/shard_map/ppermute | solution.py:44
  141.2 4.3 %collective-permute-done.16 = f32[16,4,128]{2,0,1:T(8,128)S(1)} collective-permute-done((f32[16,4,128]{2,0,1:T(8,128)S(1)}, f32[16,4,128]{2,0,1:T(8,128)S(1)}, u32[]{:S(2)}, u32[]{:S(2)}) %collective-permute-start.16) | collective-permute-done | bytes 32800 | tf_op jit(solution)/shard_map/ppermute | solution.py:44
  145.5 4.8 %collective-permute-start.18 = (f32[16,4,128]{2,0,1:T(8,128)S(1)}, f32[16,4,128]{2,0,1:T(8,128)S(1)}, u32[]{:S(2)}, u32[]{:S(2)}) collective-permute-start(f32[16,4,128]{2,0,1:T(8,128)S(1)} %fusion.74), channel_id=1, source_target_pairs={{0,2},{2,4},{4,6},{6,0},{1,3},{3,5},{5,7},{7,1},{8,10},{10,12},{12... | collective-permute-start | bytes 98312 | tf_op jit(solution)/shard_map/ppermute | solution.py:44
  152.0 4.6 %collective-permute-start.13 = (f32[32,6,256]{2,1,0:T(8,128)S(1)}, f32[32,6,256]{2,1,0:T(8,128)S(1)}, u32[]{:S(2)}, u32[]{:S(2)}) collective-permute-start(f32[32,6,256]{2,1,0:T(8,128)S(1)} %get-tuple-element.145), channel_id=1, source_target_pairs={{0,2},{2,4},{4,6},{1,3},{3,5},{5,7},{8,10},{10,12},{12,14},{9,11},... | collective-permute-start | bytes 589832 | tf_op jit(solution)/shard_map/ppermute | solution.py:35
  180.9 2.4 %fusion.132 = f32[16,24,512]{2,1,0:T(8,128)S(1)} fusion(f32[16,24,512]{2,1,0:T(8,128)S(1)} %slice_add_fusion, f32[16,24,511]{2,1,0:T(8,128)S(1)} %get-tuple-element.83, f32[16,24,511]{2,1,0:T(8,128)S(1)} %get-tuple-element.82, f32[16,23,512]{2,1,0:T(8,128)S(1)} %get-tuple-element.81, f32[16,23,512]{2,1,0:T(8,128)S(1)} %get-tuple-element.80, ...), kind=kLoop, calls=%fused_computation.215 | loop fusion | flops 5111808 | bytes 13300760 | tf_op jit(solution)/shard_map/jit(_where)/select_n | solution.py:141
  185.1 2.4 %fusion.131 = f32[16,24,512]{2,1,0:T(8,128)S(1)} fusion(f32[16,24,512]{2,1,0:T(8,128)S(1)} %fusion.132, f32[16,24,511]{2,1,0:T(8,128)S(1)} %get-tuple-element.77, f32[16,24,511]{2,1,0:T(8,128)S(1)} %get-tuple-element.76, f32[16,23,512]{2,1,0:T(8,128)S(1)} %get-tuple-element.75, f32[16,23,512]{2,1,0:T(8,128)S(1)} %get-tuple-element.74, ...), kind=kLoop, calls=%fused_computation.214 | loop fusion | flops 5111808 | bytes 13300760 | tf_op jit(solution)/shard_map/jit(_where)/select_n | solution.py:141
  189.3 2.4 %slice_multiply_fusion = (f32[16,24,512]{2,1,0:T(8,128)S(1)}, f32[16,24,512]{2,1,0:T(8,128)S(1)}) fusion(f32[16,40,512]{2,1,0:T(8,128)S(1)} %get-tuple-element.148, f32[16,24,512]{2,1,0:T(8,128)S(1)} %fusion.131, f32[16,40,512]{2,1,0:T(8,128)S(1)} %get-tuple-element.9, f32[16,24,511]{2,1,0:T(8,128)S(1)} %get-tuple-element.71, ...), kind=kLoop, calls=%fused_computation.222 | loop fusion | flops 5308416 | bytes 14087192 | tf_op jit(solution)/shard_map/mul | solution.py:89
  193.5 2.0 fusion.128
  197.2 2.5 %psum.7 = f32[16,128]{1,0:T(8,128)S(1)} all-reduce(f32[16,128]{1,0:T(8,128)S(1)} %get-tuple-element.2), channel_id=1, replica_groups=mesh['gx'=4,'gy'=4,'gz'=2] {'gz'}, use_global_device_ids=true, to_apply=%region_1.2 | all-reduce | flops 2048 | bytes 16384 | tf_op jit(solution)/shard_map/psum | solution.py:229
  (409 shorter events, 102.7 us)
Async XLA Ops:
  3.1 11.0 %collective-permute-start = (f32[34,16,128]{2,1,0:T(8,128)S(1)}, f32[34,16,128]{2,1,0:T(8,128)S(1)}, u32[]{:S(2)}, u32[]{:S(2)}) collective-permute-start(f32[34,16,128]{2,1,0:T(8,128)S(1)} %pad_maximum_fusion.4), channel_id=1, source_target_pairs={{0,24},{8,0},{16,8},{24,16},{1,25},{9,1},{17,9},{25,17},{2,26},{10... | collective-permute-start | bytes 835592 | tf_op jit(solution)/shard_map/ppermute | solution.py:44
  7.1 14.1 %collective-permute-start.1 = (f32[34,16,128]{2,1,0:T(8,128)S(1)}, f32[34,16,128]{2,1,0:T(8,128)S(1)}, u32[]{:S(2)}, u32[]{:S(2)}) collective-permute-start(f32[34,16,128]{2,1,0:T(8,128)S(1)} %pad_maximum_fusion.4), channel_id=1, source_target_pairs={{0,16},{8,24},{16,0},{24,8},{1,17},{9,25},{17,1},{25,9},{2,18},{10... | collective-permute-start | bytes 835592 | tf_op jit(solution)/shard_map/ppermute | solution.py:44
  7.6 13.6 %collective-permute-start.2 = (f32[34,16,128]{2,1,0:T(8,128)S(1)}, f32[34,16,128]{2,1,0:T(8,128)S(1)}, u32[]{:S(2)}, u32[]{:S(2)}) collective-permute-start(f32[34,16,128]{2,1,0:T(8,128)S(1)} %pad_maximum_fusion.4), channel_id=1, source_target_pairs={{0,8},{8,16},{16,24},{24,0},{1,9},{9,17},{17,25},{25,1},{2,10},{10... | collective-permute-start | bytes 835592 | tf_op jit(solution)/shard_map/ppermute | solution.py:44
  22.3 25.1 %collective-permute-start.4 = (f32[34,13,512]{2,0,1:T(8,128)S(1)}, f32[34,13,512]{2,0,1:T(8,128)S(1)}, u32[]{:S(2)}, u32[]{:S(2)}) collective-permute-start(f32[34,13,512]{2,0,1:T(8,128)S(1)} %copy.29), channel_id=1, source_target_pairs={{2,0},{4,2},{6,4},{3,1},{5,3},{7,5},{10,8},{12,10},{14,12},{11,9},... | collective-permute-start | bytes 2715656 | tf_op jit(solution)/shard_map/ppermute | solution.py:36
  25.2 25.3 %collective-permute-start.3 = (f32[34,13,512]{2,0,1:T(8,128)}, f32[34,13,512]{2,0,1:T(8,128)}, u32[]{:S(2)}, u32[]{:S(2)}) collective-permute-start(f32[34,13,512]{2,0,1:T(8,128)} %copy.28), channel_id=1, source_target_pairs={{0,2},{2,4},{4,6},{1,3},{3,5},{5,7},{8,10},{10,12},{12,14},{9,11},... | collective-permute-start | bytes 2715656 | tf_op jit(solution)/shard_map/ppermute | solution.py:35
  59.0 3.5 %collective-permute-start.5 = (f32[1,42,512]{2,1,0:T(8,128)S(1)}, f32[1,42,512]{2,1,0:T(8,128)S(1)}, u32[]{:S(2)}, u32[]{:S(2)}) collective-permute-start(f32[1,42,512]{2,1,0:T(8,128)S(1)} %maximum_select_fusion), channel_id=1, source_target_pairs={{0,1},{1,0},{2,3},{3,2},{4,5},{5,4},{6,7},{7,6},{8,9},{9,8},{10,11... | collective-permute-start | bytes 258056 | tf_op jit(solution)/shard_map/ppermute | solution.py:25
  88.5 6.9 %collective-permute-start.6 = (f32[1,40,512]{2,1,0:T(8,128)S(1)}, f32[1,40,512]{2,1,0:T(8,128)S(1)}, u32[]{:S(2)}, u32[]{:S(2)}) collective-permute-start(f32[1,40,512]{2,1,0:T(8,128)S(1)} %slice_select_fusion.3), channel_id=1, source_target_pairs={{0,1},{1,0},{2,3},{3,2},{4,5},{5,4},{6,7},{7,6},{8,9},{9,8},{10,11... | collective-permute-start | bytes 245768 | tf_op jit(solution)/shard_map/ppermute | solution.py:25
  100.1 1.3 collective-permute-start.7
  106.2 1.3 collective-permute-start.8
  112.3 1.3 collective-permute-start.9
  122.5 6.5 %collective-permute-start.10 = (f32[1,20,256]{2,1,0:T(8,128)S(1)}, f32[1,20,256]{2,1,0:T(8,128)S(1)}, u32[]{:S(2)}, u32[]{:S(2)}) collective-permute-start(f32[1,20,256]{2,1,0:T(8,128)S(1)} %slice_select_fusion.15), channel_id=1, source_target_pairs={{0,1},{1,0},{2,3},{3,2},{4,5},{5,4},{6,7},{7,6},{8,9},{9,8},{10,11... | collective-permute-start | bytes 61448 | tf_op jit(solution)/shard_map/ppermute | solution.py:25
  123.4 33.2 %collective-permute-start.19 = (f32[112,4,128]{2,0,1:T(8,128)S(1)}, f32[112,4,128]{2,0,1:T(8,128)S(1)}, u32[]{:S(2)}, u32[]{:S(2)}) collective-permute-start(f32[112,4,128]{2,0,1:T(8,128)S(1)} %fusion.63), channel_id=1, source_target_pairs={{0,6},{2,0},{4,2},{6,4},{1,7},{3,1},{5,3},{7,5},{8,14},{10,8},{12,... | collective-permute-start | bytes 688136 | tf_op jit(solution)/shard_map/ppermute | solution.py:44
  128.1 28.6 %collective-permute-start.20 = (f32[112,4,128]{2,0,1:T(8,128)S(1)}, f32[112,4,128]{2,0,1:T(8,128)S(1)}, u32[]{:S(2)}, u32[]{:S(2)}) collective-permute-start(f32[112,4,128]{2,0,1:T(8,128)S(1)} %fusion.63), channel_id=1, source_target_pairs={{0,4},{2,6},{4,0},{6,2},{1,5},{3,7},{5,1},{7,3},{8,12},{10,14},{12... | collective-permute-start | bytes 688136 | tf_op jit(solution)/shard_map/ppermute | solution.py:44
  128.1 28.7 %collective-permute-start.21 = (f32[112,4,128]{2,0,1:T(8,128)S(1)}, f32[112,4,128]{2,0,1:T(8,128)S(1)}, u32[]{:S(2)}, u32[]{:S(2)}) collective-permute-start(f32[112,4,128]{2,0,1:T(8,128)S(1)} %fusion.63), channel_id=1, source_target_pairs={{0,2},{2,4},{4,6},{6,0},{1,3},{3,5},{5,7},{7,1},{8,10},{10,12},{12... | collective-permute-start | bytes 688136 | tf_op jit(solution)/shard_map/ppermute | solution.py:44
  129.9 1.3 collective-permute-start.11
  137.1 8.4 %collective-permute-start.16 = (f32[16,4,128]{2,0,1:T(8,128)S(1)}, f32[16,4,128]{2,0,1:T(8,128)S(1)}, u32[]{:S(2)}, u32[]{:S(2)}) collective-permute-start(f32[16,4,128]{2,0,1:T(8,128)S(1)} %fusion.74), channel_id=1, source_target_pairs={{0,6},{2,0},{4,2},{6,4},{1,7},{3,1},{5,3},{7,5},{8,14},{10,8},{12,... | collective-permute-start | bytes 98312 | tf_op jit(solution)/shard_map/ppermute | solution.py:44
  140.1 10.4 %collective-permute-start.17 = (f32[16,4,128]{2,0,1:T(8,128)S(1)}, f32[16,4,128]{2,0,1:T(8,128)S(1)}, u32[]{:S(2)}, u32[]{:S(2)}) collective-permute-start(f32[16,4,128]{2,0,1:T(8,128)S(1)} %fusion.74), channel_id=1, source_target_pairs={{0,4},{2,6},{4,0},{6,2},{1,5},{3,7},{5,1},{7,3},{8,12},{10,14},{12... | collective-permute-start | bytes 98312 | tf_op jit(solution)/shard_map/ppermute | solution.py:44
  145.5 6.4 %collective-permute-start.18 = (f32[16,4,128]{2,0,1:T(8,128)S(1)}, f32[16,4,128]{2,0,1:T(8,128)S(1)}, u32[]{:S(2)}, u32[]{:S(2)}) collective-permute-start(f32[16,4,128]{2,0,1:T(8,128)S(1)} %fusion.74), channel_id=1, source_target_pairs={{0,2},{2,4},{4,6},{6,0},{1,3},{3,5},{5,7},{7,1},{8,10},{10,12},{12... | collective-permute-start | bytes 98312 | tf_op jit(solution)/shard_map/ppermute | solution.py:44
  150.5 16.8 %collective-permute-start.14 = (f32[32,6,256]{2,1,0:T(8,128)S(1)}, f32[32,6,256]{2,1,0:T(8,128)S(1)}, u32[]{:S(2)}, u32[]{:S(2)}) collective-permute-start(f32[32,6,256]{2,1,0:T(8,128)S(1)} %get-tuple-element.146), channel_id=1, source_target_pairs={{2,0},{4,2},{6,4},{3,1},{5,3},{7,5},{10,8},{12,10},{14,12},{11,9},... | collective-permute-start | bytes 589832 | tf_op jit(solution)/shard_map/ppermute | solution.py:36
  152.0 15.3 %collective-permute-start.13 = (f32[32,6,256]{2,1,0:T(8,128)S(1)}, f32[32,6,256]{2,1,0:T(8,128)S(1)}, u32[]{:S(2)}, u32[]{:S(2)}) collective-permute-start(f32[32,6,256]{2,1,0:T(8,128)S(1)} %get-tuple-element.145), channel_id=1, source_target_pairs={{0,2},{2,4},{4,6},{1,3},{3,5},{5,7},{8,10},{10,12},{12,14},{9,11},... | collective-permute-start | bytes 589832 | tf_op jit(solution)/shard_map/ppermute | solution.py:35
  179.6 1.3 collective-permute-start.33
  183.8 1.3 collective-permute-start.34
  188.0 1.3 collective-permute-start.35
  192.2 1.3 collective-permute-start.36
  (45 other events, 256.5 us)
where the time goes:
time: 203 us; the launch traced here: 201 us
  other arithmetic  53.2 us (26%)
  waiting for transfers between devices  47.8 us (24%)
  starting transfers between devices  37.6 us (19%)
  matrix products  32 us (16%)
  local copies, waits for them, and re-layouts  24.5 us (12%)
  between operations  3.07 us (2%)
  blocking collectives  2.45 us (1%)
    ppermute x24, waiting for transfers between devices, layer_halos(): got = lax.ppermute(jnp.where(first, tail, head), 'gz', [(0, 1), (1, 0)])  19.5 us
    ppermute x9, starting transfers between devices, gather_blocks(): lax.ppermute(a, axis, [(i, (i + s) % count) for i in range(count)])  19.5 us
    select_n x9, other arithmetic, sweep(): return jnp.where(inside, new, 0.0)  19 us
    dot_general x44, matrix products, cols(): return jnp.dot(a, pick(a.shape[-1], parity), precision=HI)  16.6 us
    dot_general x28, matrix products, rows(): return jnp.einsum('yr,zyx->zrx', pick(a.shape[1], parity), a, precision=HI)  13.7 us
    ppermute x9, waiting for transfers between devices, gather_blocks(): lax.ppermute(a, axis, [(i, (i + s) % count) for i in range(count)])  13.3 us
    ppermute x2, waiting for transfers between devices, extend_rows(): hi = lax.ppermute(a[:, :h], 'gy', [(i + 1, i) for i in range(count - 1)])  12.4 us
    ppermute x2, starting transfers between devices, extend_rows(): lo = lax.ppermute(a[:, -h:], 'gy', [(i, i + 1) for i in range(count - 1)])  10.3 us
  transfers between devices with their start and end apart: 37, of which 28 were waited for; matrix products, arithmetic and copies ran while one was open for 15% of the time, Pallas kernels for 0%

commit v1 on v0

--- a/solution.py
+++ b/solution.py
@@ -56,8 +56,11 @@
     return (g >= 0) & (g < own_rows * lax.axis_size("gy"))
 
 
-def neighbours(u):
-    zlo, zhi = layer_halos(u)
+def neighbours(u, whole_z=False):
+    if whole_z:
+        zlo = zhi = jnp.zeros_like(u[:1])
+    else:
+        zlo, zhi = layer_halos(u)
     zero_row = jnp.zeros_like(u[:, :1])
     zero_col = jnp.zeros_like(u[:, :, :1])
     zm = jnp.concatenate([zlo, u[:-1]], axis=0)
@@ -80,9 +83,9 @@
     return (zlo, zhi, ylo, yhi, xlo, xhi)
 
 
-def operate(u, coef):
-    zlo, zhi, ylo, yhi, xlo, xhi, extra = coef
-    zm, zp, ym, yp, xm, xp = neighbours(u)
+def operate(u, coef, whole_z=False):
+    zlo, zhi, ylo, yhi, xlo, xhi, extra = coef
+    zm, zp, ym, yp, xm, xp = neighbours(u, whole_z)
     out = zlo * (u - zm) + zhi * (u - zp)
     out = out + ylo * (u - ym) + yhi * (u - yp)
     out = out + xlo * (u - xm) + xhi * (u - xp)
@@ -136,14 +139,14 @@
     return jnp.einsum("ry,zrx->zyx", spread(field.shape[1]), wide, precision=HI)
 
 
-def sweep(field, rhs, coef, diag, inside):
-    new = field + OMEGA * (rhs - operate(field, coef)) / diag
+def sweep(field, rhs, coef, diag, inside, whole_z=False):
+    new = field + OMEGA * (rhs - operate(field, coef, whole_z)) / diag
     return jnp.where(inside, new, 0.0)
 
 
-def smooth(field, rhs, coef, diag, inside, count):
+def smooth(field, rhs, coef, diag, inside, count, whole_z=False):
     for i in range(count):
-        field = sweep(field, rhs, coef, diag, inside)
+        field = sweep(field, rhs, coef, diag, inside, whole_z)
     return field
 
 
@@ -184,7 +187,11 @@
     coarse_own = coarsen(crop_all(middle, FINE_HALO // 2, 0))
     coarse_all = gather_blocks(jnp.concatenate(coarse_own, axis=0), "gy")
     coarse_all = jnp.concatenate([coarse_all[i] for i in range(coarse_all.shape[0])], axis=1)
-    coarse = tuple(coarse_all[i * layers : (i + 1) * layers] for i in range(7))
+    coarse_all = gather_blocks(coarse_all, "gz")
+    coarse = tuple(
+        jnp.concatenate([coarse_all[k, i * layers : (i + 1) * layers] for k in range(coarse_all.shape[0])], axis=0)
+        for i in range(7)
+    )
     dcoarse = diagonal(coarse)
     in_fine = row_mask(own_rows, FINE_HALO)
     in_mid = row_mask(mid_rows, FINE_HALO // 2)
@@ -198,9 +205,12 @@
     res_mid = crop(b_mid - operate(e_mid, middle), hm, 0)
     b_low = gather_blocks(mean_four(res_mid), "gy")
     b_low = jnp.concatenate([b_low[i] for i in range(b_low.shape[0])], axis=1)
+    b_low = gather_blocks(b_low, "gz")
+    b_low = jnp.concatenate([b_low[k] for k in range(b_low.shape[0])], axis=0)
     e_low = OMEGA * b_low / dcoarse
     ones = jnp.ones((1, b_low.shape[1], 1), dtype=bool)
-    e_low = smooth(e_low, b_low, coarse, dcoarse, ones, S2 - 1)
+    e_low = smooth(e_low, b_low, coarse, dcoarse, ones, S2 - 1, whole_z=True)
+    e_low = lax.dynamic_slice_in_dim(e_low, gz * layers, layers, 0)
 
     pair = jnp.concatenate([crop(e_mid, hm, 0), crop(b_mid, hm, 0)], axis=0)
     pair = extend_rows(pair, MID_HALO)
@@ -226,7 +236,10 @@
 
     own = lax.dynamic_slice_in_dim(lam, lax.axis_index("gx") * cols_own, cols_own, 2)
     column = jnp.sum(wsq[:, None, None] * forward_velocity * own, axis=0)
-    summed = lax.psum(column, "gz")
+    parts = gather_blocks(column, "gz")
+    summed = parts[0]
+    for k in range(1, parts.shape[0]):
+        summed = summed + parts[k]
     terms = -ground_fric * summed
     gradient = lax.dynamic_slice_in_dim(terms, gz * half_cols, half_cols, 1)
     return (own, gradient)

time: 203 us -> 208 us (1.025)
  waiting for transfers between devices: 47.8 us -> 67.9 us
  other arithmetic: 53.2 us -> 45.8 us
  starting transfers between devices: 37.6 us -> 32.2 us
  blocking collectives: 2.45 us -> 0 us
    ppermute x9 -> x12, waiting for transfers between devices: 13.3 us -> 31.2 us  [gather_blocks(): lax.ppermute(a, axis, [(i, (i + s) % count) for i in range(count)])]
    ppermute x2, waiting for transfers between devices: 12.4 us -> 19.6 us  [extend_rows(): hi = lax.ppermute(a[:, :h], 'gy', [(i + 1, i) for i in range(count - 1)])]
    ppermute x24 -> x17, waiting for transfers between devices: 19.5 us -> 13.4 us  [layer_halos(): got = lax.ppermute(jnp.where(first, tail, head), 'gz', [(0, 1), (1, 0)])]
    ppermute x9 -> x12, starting transfers between devices: 19.5 us -> 15.4 us  [gather_blocks(): lax.ppermute(a, axis, [(i, (i + s) % count) for i in range(count)])]
    psum x1 -> x0, blocking collectives: 2.45 us -> none  [body_wide(): summed = lax.psum(column, 'gz')]
    div x4, other arithmetic: 2.26 us -> 0.02 us  [spread(): return (src == dst // 2).astype(jnp.float32)]
    ppermute x24 -> x17, starting transfers between devices: 5.21 us -> 3.73 us  [layer_halos(): got = lax.ppermute(jnp.where(first, tail, head), 'gz', [(0, 1), (1, 0)])]
  transfers between devices with their start and end apart: 37 -> 33, of which waited for: 28 -> 23; matrix products, arithmetic and copies ran while one was open for 15% -> 7% of each run, Pallas kernels for 0% -> 0%
where the time goes in v1:
time: 208 us; the launch traced here: 204 us
  waiting for transfers between devices  67.9 us (33%)
  other arithmetic  45.8 us (22%)
  starting transfers between devices  32.2 us (15%)
  matrix products  32 us (15%)
  local copies, waits for them, and re-layouts  23.3 us (11%)
  between operations  2.89 us (1%)
    ppermute x12, waiting for transfers between devices, gather_blocks(): lax.ppermute(a, axis, [(i, (i + s) % count) for i in range(count)])  31.2 us
    ppermute x2, waiting for transfers between devices, extend_rows(): hi = lax.ppermute(a[:, :h], 'gy', [(i + 1, i) for i in range(count - 1)])  19.6 us
    select_n x9, other arithmetic, sweep(): return jnp.where(inside, new, 0.0)  19.2 us
    dot_general x44, matrix products, cols(): return jnp.dot(a, pick(a.shape[-1], parity), precision=HI)  16.6 us
    ppermute x12, starting transfers between devices, gather_blocks(): lax.ppermute(a, axis, [(i, (i + s) % count) for i in range(count)])  15.4 us
    dot_general x28, matrix products, rows(): return jnp.einsum('yr,zyx->zrx', pick(a.shape[1], parity), a, precision=HI)  13.7 us
    ppermute x17, waiting for transfers between devices, layer_halos(): got = lax.ppermute(jnp.where(first, tail, head), 'gz', [(0, 1), (1, 0)])  13.4 us
    ppermute x2, starting transfers between devices, extend_rows(): lo = lax.ppermute(a[:, -h:], 'gy', [(i, i + 1) for i in range(count - 1)])  10.4 us
  transfers between devices with their start and end apart: 33, of which 23 were waited for; matrix products, arithmetic and copies ran while one was open for 7% of the time, Pallas kernels for 0%

profile of v1, /device:TPU:0, one launch (start us, length us, event | category | flops | bytes accessed | tf_op | source)
XLA Modules:
  0.0 204.0 jit_solution(8325096887069901064)
XLA Ops:
  3.1 3.9 %collective-permute-start = (f32[34,16,128]{2,1,0:T(8,128)S(1)}, f32[34,16,128]{2,1,0:T(8,128)S(1)}, u32[]{:S(2)}, u32[]{:S(2)}) collective-permute-start(f32[34,16,128]{2,1,0:T(8,128)S(1)} %pad_maximum_fusion.6), channel_id=1, source_target_pairs={{0,24},{8,0},{16,8},{24,16},{1,25},{9,1},{17,9},{25,17},{2,26},{10... | collective-permute-start | bytes 835592 | tf_op jit(solution)/shard_map/ppermute | solution.py:44
  8.3 5.8 %collective-permute-done = f32[34,16,128]{2,1,0:T(8,128)S(1)} collective-permute-done((f32[34,16,128]{2,1,0:T(8,128)S(1)}, f32[34,16,128]{2,1,0:T(8,128)S(1)}, u32[]{:S(2)}, u32[]{:S(2)}) %collective-permute-start) | collective-permute-done | bytes 278560 | tf_op jit(solution)/shard_map/ppermute | solution.py:44
  14.1 7.0 %collective-permute-done.1 = f32[34,16,128]{2,1,0:T(8,128)S(1)} collective-permute-done((f32[34,16,128]{2,1,0:T(8,128)S(1)}, f32[34,16,128]{2,1,0:T(8,128)S(1)}, u32[]{:S(2)}, u32[]{:S(2)}) %collective-permute-start.1) | collective-permute-done | bytes 278560 | tf_op jit(solution)/shard_map/ppermute | solution.py:44
  25.2 5.7 %collective-permute-start.3 = (f32[34,13,512]{2,0,1:T(8,128)}, f32[34,13,512]{2,0,1:T(8,128)}, u32[]{:S(2)}, u32[]{:S(2)}) collective-permute-start(f32[34,13,512]{2,0,1:T(8,128)} %copy.28), channel_id=1, source_target_pairs={{0,2},{2,4},{4,6},{1,3},{3,5},{5,7},{8,10},{10,12},{12,14},{9,11},... | collective-permute-start | bytes 2715656 | tf_op jit(solution)/shard_map/ppermute | solution.py:35
  31.6 15.8 %collective-permute-done.4 = f32[34,13,512]{2,0,1:T(8,128)S(1)} collective-permute-done((f32[34,13,512]{2,0,1:T(8,128)S(1)}, f32[34,13,512]{2,0,1:T(8,128)S(1)}, u32[]{:S(2)}, u32[]{:S(2)}) %collective-permute-start.4) | collective-permute-done | bytes 905248 | tf_op jit(solution)/shard_map/ppermute | solution.py:36
  48.0 2.5 %collective-permute-done.3 = f32[34,13,512]{2,0,1:T(8,128)} collective-permute-done((f32[34,13,512]{2,0,1:T(8,128)}, f32[34,13,512]{2,0,1:T(8,128)}, u32[]{:S(2)}, u32[]{:S(2)}) %collective-permute-start.3) | collective-permute-done | bytes 905248 | tf_op jit(solution)/shard_map/ppermute | solution.py:35
  52.7 2.1 %fusion.494 = (f32[15,42,512]{2,1,0:T(8,128)}, f32[15,42,512]{2,1,0:T(8,128)}) fusion(f32[34,42,512]{2,1,0:T(8,128)S(1)} %pad_maximum_fusion), kind=kLoop, calls=%fused_computation.721 | loop fusion | bytes 5160960 | tf_op jit(solution)/shard_map/slice | solution.py:66
  54.8 2.0 fusion.495
  56.8 2.3 %fusion.496 = (f32[16,42,511]{2,1,0:T(8,128)}, f32[16,42,511]{2,1,0:T(8,128)}) fusion(f32[34,42,512]{2,1,0:T(8,128)S(1)} %pad_maximum_fusion), kind=kLoop, calls=%fused_computation.723 | loop fusion | bytes 5494272 | tf_op jit(solution)/shard_map/slice | solution.py:70
  62.5 5.5 %fusion.3 = (f32[16,42,512]{2,1,0:T(8,128)S(1)}, f32[16,42,512]{2,1,0:T(8,128)S(1)}, f32[16,42,512]{2,1,0:T(8,128)S(1)}, f32[16,42,512]{2,1,0:T(8,128)S(1)}, f32...) fusion(f32[15,42,512]{2,1,0:T(8,128)} %get-tuple-element.16, f32[1,42,512]{2,1,0:T(8,128)S(1)} %get-tuple-element.213, ...), kind=kLoop, calls=%fused_computation.9 | loop fusion | flops 4816896 | bytes 17820416 | tf_op jit(solution)/shard_map/mul | solution.py:77
  68.0 2.4 %divide_select_fusion = (f32[16,40,512]{2,1,0:T(8,128)S(1)}, f32[16,40,512]{2,1,0:T(8,128)S(1)}) fusion(f32[34,42,512]{2,1,0:T(8,128)S(1)} %pad_maximum_fusion, pred[40]{0:T(512)(128)(4,1)S(1)} %compare_and_fusion.4, f32[16]{0:T(128)S(1)} %multiply_multiply_fusion, f32[40,512]{1,0:T(8,128)S(1)} %get-tuple-element.23, f32[40,512]{1,0:T(8,128)S(1)} %get-tuple-element.22, ...), kind=kLoop, calls=%fused_computation.69 | loop fusion | flops 3604480 | bytes 11960424 | tf_op jit(solution)/shard_map/jit(_where)/select_n | solution.py:199
  92.7 3.9 %fusion.55 = f32[16,40,512]{2,1,0:T(8,128)S(1)} fusion(f32[16,40,512]{2,1,0:T(8,128)S(1)} %get-tuple-element.9, f32[16,40,511]{2,1,0:T(8,128)S(1)} %get-tuple-element.71, f32[16,40,511]{2,1,0:T(8,128)S(1)} %get-tuple-element.70, f32[16,39,512]{2,1,0:T(8,128)S(1)} %get-tuple-element.69, f32[16,39,512]{2,1,0:T(8,128)S(1)} %get-tuple-element.68, ...), kind=kLoop, calls=%fused_computation.76 | loop fusion | flops 10158080 | bytes 19754088 | tf_op jit(solution)/shard_map/jit(_where)/select_n | solution.py:144
  98.8 4.0 %fusion.54 = f32[16,40,512]{2,1,0:T(8,128)S(1)} fusion(f32[16,40,512]{2,1,0:T(8,128)S(1)} %fusion.55, f32[16,40,512]{2,1,0:T(8,128)S(1)} %get-tuple-element.9, f32[16,40,511]{2,1,0:T(8,128)S(1)} %get-tuple-element.65, f32[16,40,511]{2,1,0:T(8,128)S(1)} %get-tuple-element.64, f32[16,39,512]{2,1,0:T(8,128)S(1)} %get-tuple-element.63, ...), kind=kLoop, calls=%fused_computation.75 | loop fusion | flops 9175040 | bytes 21064808 | tf_op jit(solution)/shard_map/jit(_where)/select_n | solution.py:144
  104.9 4.0 %fusion.53 = f32[16,40,512]{2,1,0:T(8,128)S(1)} fusion(f32[16,40,512]{2,1,0:T(8,128)S(1)} %fusion.54, f32[16,40,512]{2,1,0:T(8,128)S(1)} %get-tuple-element.9, f32[16,40,511]{2,1,0:T(8,128)S(1)} %get-tuple-element.59, f32[16,40,511]{2,1,0:T(8,128)S(1)} %get-tuple-element.58, f32[16,39,512]{2,1,0:T(8,128)S(1)} %get-tuple-element.57, ...), kind=kLoop, calls=%fused_computation.74 | loop fusion | flops 9175040 | bytes 21064808 | tf_op jit(solution)/shard_map/jit(_where)/select_n | solution.py:144
  111.0 3.6 %fusion.48 = (f32[16,40,512]{2,1,0:T(8,128)S(1)}, f32[16,40,512]{2,1,0:T(8,128)S(1)}) fusion(f32[16,40,512]{2,1,0:T(8,128)S(1)} %fusion.53, f32[15,40,512]{2,1,0:T(8,128)S(1)} %get-tuple-element.53, f32[1,40,512]{2,1,0:T(8,128)S(1)} %get-tuple-element.216, f32[1,40,512]{2,1,0:T(8,128)S(1)} %get-tuple-element.215, f32[15,40,512]{2,1,0:T(8,128)S(1)} %get-tuple-element.52, ...), kind=kLoop, calls=%fused_computation.66 | loop fusion | flops 7864320 | bytes 21064768 | tf_op jit(solution)/shard_map/sub | solution.py:201
  129.2 4.6 %collective-permute-start.16 = (f32[16,4,128]{2,0,1:T(8,128)S(1)}, f32[16,4,128]{2,0,1:T(8,128)S(1)}, u32[]{:S(2)}, u32[]{:S(2)}) collective-permute-start(f32[16,4,128]{2,0,1:T(8,128)S(1)} %fusion.77), channel_id=1, source_target_pairs={{0,6},{2,0},{4,2},{6,4},{1,7},{3,1},{5,3},{7,5},{8,14},{10,8},{12,... | collective-permute-start | bytes 98312 | tf_op jit(solution)/shard_map/ppermute | solution.py:44
  136.0 2.9 %collective-permute-start.17 = (f32[16,4,128]{2,0,1:T(8,128)S(1)}, f32[16,4,128]{2,0,1:T(8,128)S(1)}, u32[]{:S(2)}, u32[]{:S(2)}) collective-permute-start(f32[16,4,128]{2,0,1:T(8,128)S(1)} %fusion.77), channel_id=1, source_target_pairs={{0,4},{2,6},{4,0},{6,2},{1,5},{3,7},{5,1},{7,3},{8,12},{10,14},{12... | collective-permute-start | bytes 98312 | tf_op jit(solution)/shard_map/ppermute | solution.py:44
  139.0 17.4 %collective-permute-done.17 = f32[16,4,128]{2,0,1:T(8,128)S(1)} collective-permute-done((f32[16,4,128]{2,0,1:T(8,128)S(1)}, f32[16,4,128]{2,0,1:T(8,128)S(1)}, u32[]{:S(2)}, u32[]{:S(2)}) %collective-permute-start.17) | collective-permute-done | bytes 32800 | tf_op jit(solution)/shard_map/ppermute | solution.py:44
  158.9 4.7 %collective-permute-start.13 = (f32[32,6,256]{2,1,0:T(8,128)S(1)}, f32[32,6,256]{2,1,0:T(8,128)S(1)}, u32[]{:S(2)}, u32[]{:S(2)}) collective-permute-start(f32[32,6,256]{2,1,0:T(8,128)S(1)} %get-tuple-element.207), channel_id=1, source_target_pairs={{0,2},{2,4},{4,6},{1,3},{3,5},{5,7},{8,10},{10,12},{12,14},{9,11},... | collective-permute-start | bytes 589832 | tf_op jit(solution)/shard_map/ppermute | solution.py:35
  163.9 3.9 %collective-permute-done.14 = f32[32,6,256]{2,1,0:T(8,128)S(1)} collective-permute-done((f32[32,6,256]{2,1,0:T(8,128)S(1)}, f32[32,6,256]{2,1,0:T(8,128)S(1)}, u32[]{:S(2)}, u32[]{:S(2)}) %collective-permute-start.14) | collective-permute-done | bytes 196640 | tf_op jit(solution)/shard_map/ppermute | solution.py:36
  186.3 2.6 %fusion.135 = f32[16,24,512]{2,1,0:T(8,128)S(1)} fusion(f32[16,24,512]{2,1,0:T(8,128)S(1)} %slice_add_fusion, f32[16,24,511]{2,1,0:T(8,128)S(1)} %get-tuple-element.99, f32[16,24,511]{2,1,0:T(8,128)S(1)} %get-tuple-element.98, f32[16,23,512]{2,1,0:T(8,128)S(1)} %get-tuple-element.97, f32[16,23,512]{2,1,0:T(8,128)S(1)} %get-tuple-element.96, ...), kind=kLoop, calls=%fused_computation.222 | loop fusion | flops 5111808 | bytes 13300760 | tf_op jit(solution)/shard_map/jit(_where)/select_n | solution.py:144
  190.7 2.4 %fusion.134 = f32[16,24,512]{2,1,0:T(8,128)S(1)} fusion(f32[16,24,512]{2,1,0:T(8,128)S(1)} %fusion.135, f32[16,24,511]{2,1,0:T(8,128)S(1)} %get-tuple-element.93, f32[16,24,511]{2,1,0:T(8,128)S(1)} %get-tuple-element.92, f32[16,23,512]{2,1,0:T(8,128)S(1)} %get-tuple-element.91, f32[16,23,512]{2,1,0:T(8,128)S(1)} %get-tuple-element.90, ...), kind=kLoop, calls=%fused_computation.221 | loop fusion | flops 5111808 | bytes 13300760 | tf_op jit(solution)/shard_map/jit(_where)/select_n | solution.py:144
  194.9 2.4 %slice_multiply_fusion = (f32[16,24,512]{2,1,0:T(8,128)S(1)}, f32[16,24,512]{2,1,0:T(8,128)S(1)}) fusion(f32[16,40,512]{2,1,0:T(8,128)S(1)} %get-tuple-element.210, f32[16,24,512]{2,1,0:T(8,128)S(1)} %fusion.134, f32[16,40,512]{2,1,0:T(8,128)S(1)} %get-tuple-element.9, f32[16,24,511]{2,1,0:T(8,128)S(1)} %get-tuple-element.87, ...), kind=kLoop, calls=%fused_computation.229 | loop fusion | flops 5308416 | bytes 14087192 | tf_op jit(solution)/shard_map/mul | solution.py:92
  199.1 2.0 fusion.131
  (342 shorter events, 87.9 us)
Async XLA Ops:
  3.1 11.0 %collective-permute-start = (f32[34,16,128]{2,1,0:T(8,128)S(1)}, f32[34,16,128]{2,1,0:T(8,128)S(1)}, u32[]{:S(2)}, u32[]{:S(2)}) collective-permute-start(f32[34,16,128]{2,1,0:T(8,128)S(1)} %pad_maximum_fusion.6), channel_id=1, source_target_pairs={{0,24},{8,0},{16,8},{24,16},{1,25},{9,1},{17,9},{25,17},{2,26},{10... | collective-permute-start | bytes 835592 | tf_op jit(solution)/shard_map/ppermute | solution.py:44
  7.1 14.1 %collective-permute-start.1 = (f32[34,16,128]{2,1,0:T(8,128)S(1)}, f32[34,16,128]{2,1,0:T(8,128)S(1)}, u32[]{:S(2)}, u32[]{:S(2)}) collective-permute-start(f32[34,16,128]{2,1,0:T(8,128)S(1)} %pad_maximum_fusion.6), channel_id=1, source_target_pairs={{0,16},{8,24},{16,0},{24,8},{1,17},{9,25},{17,1},{25,9},{2,18},{10... | collective-permute-start | bytes 835592 | tf_op jit(solution)/shard_map/ppermute | solution.py:44
  7.6 13.6 %collective-permute-start.2 = (f32[34,16,128]{2,1,0:T(8,128)S(1)}, f32[34,16,128]{2,1,0:T(8,128)S(1)}, u32[]{:S(2)}, u32[]{:S(2)}) collective-permute-start(f32[34,16,128]{2,1,0:T(8,128)S(1)} %pad_maximum_fusion.6), channel_id=1, source_target_pairs={{0,8},{8,16},{16,24},{24,0},{1,9},{9,17},{17,25},{25,1},{2,10},{10... | collective-permute-start | bytes 835592 | tf_op jit(solution)/shard_map/ppermute | solution.py:44
  22.4 25.1 %collective-permute-start.4 = (f32[34,13,512]{2,0,1:T(8,128)S(1)}, f32[34,13,512]{2,0,1:T(8,128)S(1)}, u32[]{:S(2)}, u32[]{:S(2)}) collective-permute-start(f32[34,13,512]{2,0,1:T(8,128)S(1)} %copy.29), channel_id=1, source_target_pairs={{2,0},{4,2},{6,4},{3,1},{5,3},{7,5},{10,8},{12,10},{14,12},{11,9},... | collective-permute-start | bytes 2715656 | tf_op jit(solution)/shard_map/ppermute | solution.py:36
  25.2 25.3 %collective-permute-start.3 = (f32[34,13,512]{2,0,1:T(8,128)}, f32[34,13,512]{2,0,1:T(8,128)}, u32[]{:S(2)}, u32[]{:S(2)}) collective-permute-start(f32[34,13,512]{2,0,1:T(8,128)} %copy.28), channel_id=1, source_target_pairs={{0,2},{2,4},{4,6},{1,3},{3,5},{5,7},{8,10},{10,12},{12,14},{9,11},... | collective-permute-start | bytes 2715656 | tf_op jit(solution)/shard_map/ppermute | solution.py:35
  59.1 3.4 %collective-permute-start.5 = (f32[1,42,512]{2,1,0:T(8,128)S(1)}, f32[1,42,512]{2,1,0:T(8,128)S(1)}, u32[]{:S(2)}, u32[]{:S(2)}) collective-permute-start(f32[1,42,512]{2,1,0:T(8,128)S(1)} %maximum_select_fusion), channel_id=1, source_target_pairs={{0,1},{1,0},{2,3},{3,2},{4,5},{5,4},{6,7},{7,6},{8,9},{9,8},{10,11... | collective-permute-start | bytes 258056 | tf_op jit(solution)/shard_map/ppermute | solution.py:25
  86.8 6.0 %collective-permute-start.6 = (f32[1,40,512]{2,1,0:T(8,128)S(1)}, f32[1,40,512]{2,1,0:T(8,128)S(1)}, u32[]{:S(2)}, u32[]{:S(2)}) collective-permute-start(f32[1,40,512]{2,1,0:T(8,128)S(1)} %slice_select_fusion.3), channel_id=1, source_target_pairs={{0,1},{1,0},{2,3},{3,2},{4,5},{5,4},{6,7},{7,6},{8,9},{9,8},{10,11... | collective-permute-start | bytes 245768 | tf_op jit(solution)/shard_map/ppermute | solution.py:25
  97.4 1.3 collective-permute-start.7
  103.5 1.3 collective-permute-start.8
  109.7 1.3 collective-permute-start.9
  129.2 9.8 %collective-permute-start.16 = (f32[16,4,128]{2,0,1:T(8,128)S(1)}, f32[16,4,128]{2,0,1:T(8,128)S(1)}, u32[]{:S(2)}, u32[]{:S(2)}) collective-permute-start(f32[16,4,128]{2,0,1:T(8,128)S(1)} %fusion.77), channel_id=1, source_target_pairs={{0,6},{2,0},{4,2},{6,4},{1,7},{3,1},{5,3},{7,5},{8,14},{10,8},{12,... | collective-permute-start | bytes 98312 | tf_op jit(solution)/shard_map/ppermute | solution.py:44
  134.0 22.5 %collective-permute-start.20 = (f32[112,4,128]{2,0,1:T(8,128)S(1)}, f32[112,4,128]{2,0,1:T(8,128)S(1)}, u32[]{:S(2)}, u32[]{:S(2)}) collective-permute-start(f32[112,4,128]{2,0,1:T(8,128)S(1)} %fusion.66), channel_id=1, source_target_pairs={{0,6},{2,0},{4,2},{6,4},{1,7},{3,1},{5,3},{7,5},{8,14},{10,8},{12,... | collective-permute-start | bytes 688136 | tf_op jit(solution)/shard_map/ppermute | solution.py:44
  134.4 22.1 %collective-permute-start.21 = (f32[112,4,128]{2,0,1:T(8,128)S(1)}, f32[112,4,128]{2,0,1:T(8,128)S(1)}, u32[]{:S(2)}, u32[]{:S(2)}) collective-permute-start(f32[112,4,128]{2,0,1:T(8,128)S(1)} %fusion.66), channel_id=1, source_target_pairs={{0,4},{2,6},{4,0},{6,2},{1,5},{3,7},{5,1},{7,3},{8,12},{10,14},{12... | collective-permute-start | bytes 688136 | tf_op jit(solution)/shard_map/ppermute | solution.py:44
  134.4 22.1 %collective-permute-start.22 = (f32[112,4,128]{2,0,1:T(8,128)S(1)}, f32[112,4,128]{2,0,1:T(8,128)S(1)}, u32[]{:S(2)}, u32[]{:S(2)}) collective-permute-start(f32[112,4,128]{2,0,1:T(8,128)S(1)} %fusion.66), channel_id=1, source_target_pairs={{0,2},{2,4},{4,6},{6,0},{1,3},{3,5},{5,7},{7,1},{8,10},{10,12},{12... | collective-permute-start | bytes 688136 | tf_op jit(solution)/shard_map/ppermute | solution.py:44
  136.0 20.3 %collective-permute-start.17 = (f32[16,4,128]{2,0,1:T(8,128)S(1)}, f32[16,4,128]{2,0,1:T(8,128)S(1)}, u32[]{:S(2)}, u32[]{:S(2)}) collective-permute-start(f32[16,4,128]{2,0,1:T(8,128)S(1)} %fusion.77), channel_id=1, source_target_pairs={{0,4},{2,6},{4,0},{6,2},{1,5},{3,7},{5,1},{7,3},{8,12},{10,14},{12... | collective-permute-start | bytes 98312 | tf_op jit(solution)/shard_map/ppermute | solution.py:44
  139.0 17.4 %collective-permute-start.18 = (f32[16,4,128]{2,0,1:T(8,128)S(1)}, f32[16,4,128]{2,0,1:T(8,128)S(1)}, u32[]{:S(2)}, u32[]{:S(2)}) collective-permute-start(f32[16,4,128]{2,0,1:T(8,128)S(1)} %fusion.77), channel_id=1, source_target_pairs={{0,2},{2,4},{4,6},{6,0},{1,3},{3,5},{5,7},{7,1},{8,10},{10,12},{12... | collective-permute-start | bytes 98312 | tf_op jit(solution)/shard_map/ppermute | solution.py:44
  156.9 12.2 %collective-permute-start.23 = (f32[112,16,128]{2,0,1:T(8,128)S(1)}, f32[112,16,128]{2,0,1:T(8,128)S(1)}, u32[]{:S(2)}, u32[]{:S(2)}) collective-permute-start(f32[112,16,128]{2,0,1:T(8,128)S(1)} %get-tuple-element.75), channel_id=1, source_target_pairs={{0,1},{1,0},{2,3},{3,2},{4,5},{5,4},{6,7},{7,6},{8,9},{9,8},{10,11... | collective-permute-start | bytes 2752520 | tf_op jit(solution)/shard_map/ppermute | solution.py:44
  157.0 6.8 %collective-permute-start.19 = (f32[16,16,128]{2,0,1:T(8,128)S(1)}, f32[16,16,128]{2,0,1:T(8,128)S(1)}, u32[]{:S(2)}, u32[]{:S(2)}) collective-permute-start(f32[16,16,128]{2,0,1:T(8,128)S(1)} %get-tuple-element.212), channel_id=1, source_target_pairs={{0,1},{1,0},{2,3},{3,2},{4,5},{5,4},{6,7},{7,6},{8,9},{9,8},{10,11... | collective-permute-start | bytes 393224 | tf_op jit(solution)/shard_map/ppermute | solution.py:44
  157.6 10.1 %collective-permute-start.14 = (f32[32,6,256]{2,1,0:T(8,128)S(1)}, f32[32,6,256]{2,1,0:T(8,128)S(1)}, u32[]{:S(2)}, u32[]{:S(2)}) collective-permute-start(f32[32,6,256]{2,1,0:T(8,128)S(1)} %get-tuple-element.208), channel_id=1, source_target_pairs={{2,0},{4,2},{6,4},{3,1},{5,3},{7,5},{10,8},{12,10},{14,12},{11,9},... | collective-permute-start | bytes 589832 | tf_op jit(solution)/shard_map/ppermute | solution.py:36
  158.9 10.0 %collective-permute-start.13 = (f32[32,6,256]{2,1,0:T(8,128)S(1)}, f32[32,6,256]{2,1,0:T(8,128)S(1)}, u32[]{:S(2)}, u32[]{:S(2)}) collective-permute-start(f32[32,6,256]{2,1,0:T(8,128)S(1)} %get-tuple-element.207), channel_id=1, source_target_pairs={{0,2},{2,4},{4,6},{1,3},{3,5},{5,7},{8,10},{10,12},{12,14},{9,11},... | collective-permute-start | bytes 589832 | tf_op jit(solution)/shard_map/ppermute | solution.py:35
  185.0 1.3 collective-permute-start.28
  189.4 1.3 collective-permute-start.29
  193.5 1.3 collective-permute-start.30
  197.8 1.3 collective-permute-start.31
  (15 other events, 77.9 us)

commit v2 on v1

--- a/solution.py
+++ b/solution.py
@@ -185,14 +185,6 @@
     middle = coarsen(fine)
     dmid = diagonal(middle)
     coarse_own = coarsen(crop_all(middle, FINE_HALO // 2, 0))
-    coarse_all = gather_blocks(jnp.concatenate(coarse_own, axis=0), "gy")
-    coarse_all = jnp.concatenate([coarse_all[i] for i in range(coarse_all.shape[0])], axis=1)
-    coarse_all = gather_blocks(coarse_all, "gz")
-    coarse = tuple(
-        jnp.concatenate([coarse_all[k, i * layers : (i + 1) * layers] for k in range(coarse_all.shape[0])], axis=0)
-        for i in range(7)
-    )
-    dcoarse = diagonal(coarse)
     in_fine = row_mask(own_rows, FINE_HALO)
     in_mid = row_mask(mid_rows, FINE_HALO // 2)
 
@@ -203,10 +195,16 @@
     e_mid = smooth(e_mid, b_mid, middle, dmid, in_mid, S1 - 1)
     hm = FINE_HALO // 2
     res_mid = crop(b_mid - operate(e_mid, middle), hm, 0)
-    b_low = gather_blocks(mean_four(res_mid), "gy")
-    b_low = jnp.concatenate([b_low[i] for i in range(b_low.shape[0])], axis=1)
-    b_low = gather_blocks(b_low, "gz")
-    b_low = jnp.concatenate([b_low[k] for k in range(b_low.shape[0])], axis=0)
+    low_all = gather_blocks(jnp.concatenate(coarse_own + (mean_four(res_mid),), axis=0), "gy")
+    low_all = jnp.concatenate([low_all[i] for i in range(low_all.shape[0])], axis=1)
+    low_all = gather_blocks(low_all, "gz")
+    low_all = tuple(
+        jnp.concatenate([low_all[k, i * layers : (i + 1) * layers] for k in range(low_all.shape[0])], axis=0)
+        for i in range(8)
+    )
+    coarse = low_all[:7]
+    b_low = low_all[7]
+    dcoarse = diagonal(coarse)
     e_low = OMEGA * b_low / dcoarse
     ones = jnp.ones((1, b_low.shape[1], 1), dtype=bool)
     e_low = smooth(e_low, b_low, coarse, dcoarse, ones, S2 - 1, whole_z=True)

time: 208 us -> 228 us (1.096)
  local copies, waits for them, and re-layouts: 23.3 us -> 30.9 us
  matrix products: 32 us -> 38.5 us
  other arithmetic: 45.8 us -> 51.8 us
  waiting for transfers between devices: 67.9 us -> 73.7 us
  starting transfers between devices: 32.2 us -> 26.8 us
    unnamed x32 -> x113, local copies, waits for them, and re-layouts: 0.31 us -> 9.85 us
    dot_general x44, matrix products: 16.6 us -> 23 us  [cols(): return jnp.dot(a, pick(a.shape[-1], parity), precision=HI)]
    ppermute x12 -> x8, starting transfers between devices: 15.4 us -> 10.6 us  [gather_blocks(): lax.ppermute(a, axis, [(i, (i + s) % count) for i in range(count)])]
    ppermute x12 -> x8, waiting for transfers between devices: 31.2 us -> 35.3 us  [gather_blocks(): lax.ppermute(a, axis, [(i, (i + s) % count) for i in range(count)])]
  transfers between devices with their start and end apart: 33 -> 29, of which waited for: 23 -> 23; matrix products, arithmetic and copies ran while one was open for 7% -> 10% of each run, Pallas kernels for 0% -> 0%
where the time goes in v2:
time: 228 us; the launch traced here: 225 us
  waiting for transfers between devices  73.7 us (32%)
  other arithmetic  51.8 us (23%)
  matrix products  38.5 us (17%)
  local copies, waits for them, and re-layouts  30.9 us (14%)
  starting transfers between devices  26.8 us (12%)
  between operations  3.17 us (1%)
    ppermute x8, waiting for transfers between devices, gather_blocks(): lax.ppermute(a, axis, [(i, (i + s) % count) for i in range(count)])  35.3 us
    dot_general x44, matrix products, cols(): return jnp.dot(a, pick(a.shape[-1], parity), precision=HI)  23 us
    ppermute x2, waiting for transfers between devices, extend_rows(): hi = lax.ppermute(a[:, :h], 'gy', [(i + 1, i) for i in range(count - 1)])  21.7 us
    select_n x9, other arithmetic, sweep(): return jnp.where(inside, new, 0.0)  19 us
    dot_general x28, matrix products, rows(): return jnp.einsum('yr,zyx->zrx', pick(a.shape[1], parity), a, precision=HI)  13.7 us
    ppermute x17, waiting for transfers between devices, layer_halos(): got = lax.ppermute(jnp.where(first, tail, head), 'gz', [(0, 1), (1, 0)])  13 us
    ppermute x8, starting transfers between devices, gather_blocks(): lax.ppermute(a, axis, [(i, (i + s) % count) for i in range(count)])  10.6 us
    unnamed x113, local copies, waits for them, and re-layouts  9.85 us
  transfers between devices with their start and end apart: 29, of which 23 were waited for; matrix products, arithmetic and copies ran while one was open for 10% of the time, Pallas kernels for 0%

profile of v2, /device:TPU:0, one launch (start us, length us, event | category | flops | bytes accessed | tf_op | source)
XLA Modules:
  0.0 224.8 jit_solution(11546570889245427119)
XLA Ops:
  2.1 1.7 pad_maximum_fusion.6
  3.8 3.9 %collective-permute-start = (f32[34,16,128]{2,1,0:T(8,128)}, f32[34,16,128]{2,1,0:T(8,128)S(1)}, u32[]{:S(2)}, u32[]{:S(2)}) collective-permute-start(f32[34,16,128]{2,1,0:T(8,128)} %pad_maximum_fusion.6), channel_id=1, source_target_pairs={{0,24},{8,0},{16,8},{24,16},{1,25},{9,1},{17,9},{25,17},{2,26},{10... | collective-permute-start | bytes 835592 | tf_op jit(solution)/shard_map/ppermute | solution.py:44
  8.8 6.3 %collective-permute-done = f32[34,16,128]{2,1,0:T(8,128)S(1)} collective-permute-done((f32[34,16,128]{2,1,0:T(8,128)}, f32[34,16,128]{2,1,0:T(8,128)S(1)}, u32[]{:S(2)}, u32[]{:S(2)}) %collective-permute-start) | collective-permute-done | bytes 278560 | tf_op jit(solution)/shard_map/ppermute | solution.py:44
  15.1 6.9 %collective-permute-done.1 = f32[34,16,128]{2,1,0:T(8,128)S(1)} collective-permute-done((f32[34,16,128]{2,1,0:T(8,128)}, f32[34,16,128]{2,1,0:T(8,128)S(1)}, u32[]{:S(2)}, u32[]{:S(2)}) %collective-permute-start.1) | collective-permute-done | bytes 278560 | tf_op jit(solution)/shard_map/ppermute | solution.py:44
  27.1 4.8 %collective-permute-start.3 = (f32[34,13,512]{2,0,1:T(8,128)}, f32[34,13,512]{2,0,1:T(8,128)S(1)}, u32[]{:S(2)}, u32[]{:S(2)}) collective-permute-start(f32[34,13,512]{2,0,1:T(8,128)} %copy.28), channel_id=1, source_target_pairs={{0,2},{2,4},{4,6},{1,3},{3,5},{5,7},{8,10},{10,12},{12,14},{9,11},... | collective-permute-start | bytes 2715656 | tf_op jit(solution)/shard_map/ppermute | solution.py:35
  32.0 17.3 %collective-permute-done.4 = f32[34,13,512]{2,0,1:T(8,128)S(1)} collective-permute-done((f32[34,13,512]{2,0,1:T(8,128)S(1)}, f32[34,13,512]{2,0,1:T(8,128)S(1)}, u32[]{:S(2)}, u32[]{:S(2)}) %collective-permute-start.4) | collective-permute-done | bytes 905248 | tf_op jit(solution)/shard_map/ppermute | solution.py:36
  49.9 2.4 %collective-permute-done.3 = f32[34,13,512]{2,0,1:T(8,128)S(1)} collective-permute-done((f32[34,13,512]{2,0,1:T(8,128)}, f32[34,13,512]{2,0,1:T(8,128)S(1)}, u32[]{:S(2)}, u32[]{:S(2)}) %collective-permute-start.3) | collective-permute-done | bytes 905248 | tf_op jit(solution)/shard_map/ppermute | solution.py:35
  53.4 2.1 fusion.489
  57.1 2.2 fusion.491
  64.1 5.0 %fusion.3 = (f32[16,42,512]{2,1,0:T(8,128)S(1)}, f32[16,42,512]{2,1,0:T(8,128)S(1)}, f32[16,42,512]{2,1,0:T(8,128)S(1)}, f32[16,42,512]{2,1,0:T(8,128)S(1)}, f32...) fusion(f32[15,42,512]{2,1,0:T(8,128)} %get-tuple-element.16, f32[1,42,512]{2,1,0:T(8,128)S(1)} %get-tuple-element.207, ...), kind=kLoop, calls=%fused_computation.9 | loop fusion | flops 4816896 | bytes 17820416 | tf_op jit(solution)/shard_map/mul | solution.py:77
  69.2 2.5 %divide_select_fusion = (f32[16,40,512]{2,1,0:T(8,128)S(1)}, f32[16,40,512]{2,1,0:T(8,128)S(1)}) fusion(f32[34,42,512]{2,1,0:T(8,128)S(1)} %pad_maximum_fusion, pred[40]{0:T(512)(128)(4,1)S(1)} %compare_and_fusion.4, f32[16]{0:T(128)S(1)} %multiply_multiply_fusion, f32[40,512]{1,0:T(8,128)S(1)} %get-tuple-element.23, f32[40,512]{1,0:T(8,128)S(1)} %get-tuple-element.22, ...), kind=kLoop, calls=%fused_computation.69 | loop fusion | flops 3604480 | bytes 11960424 | tf_op jit(solution)/shard_map/jit(_where)/select_n | solution.py:191
  97.7 3.8 %fusion.55 = f32[16,40,512]{2,1,0:T(8,128)S(1)} fusion(f32[16,40,512]{2,1,0:T(8,128)S(1)} %get-tuple-element.9, f32[16,40,511]{2,1,0:T(8,128)S(1)} %get-tuple-element.73, f32[16,40,511]{2,1,0:T(8,128)S(1)} %get-tuple-element.72, f32[16,39,512]{2,1,0:T(8,128)S(1)} %get-tuple-element.71, f32[16,39,512]{2,1,0:T(8,128)S(1)} %get-tuple-element.70, ...), kind=kLoop, calls=%fused_computation.76 | loop fusion | flops 10158080 | bytes 19754088 | tf_op jit(solution)/shard_map/jit(_where)/select_n | solution.py:144
  103.7 3.9 %fusion.54 = f32[16,40,512]{2,1,0:T(8,128)S(1)} fusion(f32[16,40,512]{2,1,0:T(8,128)S(1)} %fusion.55, f32[16,40,512]{2,1,0:T(8,128)S(1)} %get-tuple-element.9, f32[16,40,511]{2,1,0:T(8,128)S(1)} %get-tuple-element.67, f32[16,40,511]{2,1,0:T(8,128)S(1)} %get-tuple-element.66, f32[16,39,512]{2,1,0:T(8,128)S(1)} %get-tuple-element.65, ...), kind=kLoop, calls=%fused_computation.75 | loop fusion | flops 9175040 | bytes 21064808 | tf_op jit(solution)/shard_map/jit(_where)/select_n | solution.py:144
  109.9 3.9 %fusion.53 = f32[16,40,512]{2,1,0:T(8,128)S(1)} fusion(f32[16,40,512]{2,1,0:T(8,128)S(1)} %fusion.54, f32[16,40,512]{2,1,0:T(8,128)S(1)} %get-tuple-element.9, f32[16,40,511]{2,1,0:T(8,128)S(1)} %get-tuple-element.61, f32[16,40,511]{2,1,0:T(8,128)S(1)} %get-tuple-element.60, f32[16,39,512]{2,1,0:T(8,128)S(1)} %get-tuple-element.59, ...), kind=kLoop, calls=%fused_computation.74 | loop fusion | flops 9175040 | bytes 21064808 | tf_op jit(solution)/shard_map/jit(_where)/select_n | solution.py:144
  116.1 4.4 %fusion.48 = (f32[16,40,512]{2,1,0:T(8,128)S(1)}, f32[16,40,512]{2,1,0:T(8,128)}) fusion(f32[16,40,512]{2,1,0:T(8,128)S(1)} %fusion.53, f32[15,40,512]{2,1,0:T(8,128)S(1)} %get-tuple-element.55, f32[1,40,512]{2,1,0:T(8,128)S(1)} %get-tuple-element.210, f32[1,40,512]{2,1,0:T(8,128)S(1)} %get-tuple-element.209, f32[15,40,512]{2,1,0:T(8,128)S(1)} %get-tuple-element.54, ...), kind=kLoop, calls=%fused_computation.66 | loop fusion | flops 7864320 | bytes 21064768 | tf_op jit(solution)/shard_map/sub | solution.py:193
  137.4 4.5 %collective-permute-start.16 = (f32[128,4,128]{2,0,1:T(8,128)}, f32[128,4,128]{2,0,1:T(8,128)}, u32[]{:S(2)}, u32[]{:S(2)}) collective-permute-start(f32[128,4,128]{2,0,1:T(8,128)} %fusion.66), channel_id=1, source_target_pairs={{0,6},{2,0},{4,2},{6,4},{1,7},{3,1},{5,3},{7,5},{8,14},{10,8},{12,... | collective-permute-start | bytes 786440 | tf_op jit(solution)/shard_map/ppermute | solution.py:44
  142.8 6.1 %collective-permute-done.16 = f32[128,4,128]{2,0,1:T(8,128)} collective-permute-done((f32[128,4,128]{2,0,1:T(8,128)}, f32[128,4,128]{2,0,1:T(8,128)}, u32[]{:S(2)}, u32[]{:S(2)}) %collective-permute-start.16) | collective-permute-done | bytes 262176 | tf_op jit(solution)/shard_map/ppermute | solution.py:44
  149.9 15.1 %collective-permute-done.17 = f32[128,4,128]{2,0,1:T(8,128)} collective-permute-done((f32[128,4,128]{2,0,1:T(8,128)}, f32[128,4,128]{2,0,1:T(8,128)}, u32[]{:S(2)}, u32[]{:S(2)}) %collective-permute-start.17) | collective-permute-done | bytes 262176 | tf_op jit(solution)/shard_map/ppermute | solution.py:44
  174.2 4.7 %collective-permute-start.13 = (f32[32,6,256]{2,1,0:T(8,128)S(1)}, f32[32,6,256]{2,1,0:T(8,128)S(1)}, u32[]{:S(2)}, u32[]{:S(2)}) collective-permute-start(f32[32,6,256]{2,1,0:T(8,128)S(1)} %get-tuple-element.203), channel_id=1, source_target_pairs={{0,2},{2,4},{4,6},{1,3},{3,5},{5,7},{8,10},{10,12},{12,14},{9,11},... | collective-permute-start | bytes 589832 | tf_op jit(solution)/shard_map/ppermute | solution.py:35
  179.1 4.4 %collective-permute-done.14 = f32[32,6,256]{2,1,0:T(8,128)S(1)} collective-permute-done((f32[32,6,256]{2,1,0:T(8,128)S(1)}, f32[32,6,256]{2,1,0:T(8,128)S(1)}, u32[]{:S(2)}, u32[]{:S(2)}) %collective-permute-start.14) | collective-permute-done | bytes 196640 | tf_op jit(solution)/shard_map/ppermute | solution.py:36
  207.1 2.6 %fusion.136 = f32[16,24,512]{2,1,0:T(8,128)S(1)} fusion(f32[16,24,512]{2,1,0:T(8,128)S(1)} %slice_add_fusion, f32[16,24,511]{2,1,0:T(8,128)S(1)} %get-tuple-element.101, f32[16,24,511]{2,1,0:T(8,128)S(1)} %get-tuple-element.100, f32[16,23,512]{2,1,0:T(8,128)S(1)} %get-tuple-element.99, f32[16,23,512]{2,1,0:T(8,128)S(1)} %get-tuple-element.98, ...), kind=kLoop, calls=%fused_computation.223 | loop fusion | flops 5111808 | bytes 13300760 | tf_op jit(solution)/shard_map/jit(_where)/select_n | solution.py:144
  211.5 2.4 %fusion.135 = f32[16,24,512]{2,1,0:T(8,128)S(1)} fusion(f32[16,24,512]{2,1,0:T(8,128)S(1)} %fusion.136, f32[16,24,511]{2,1,0:T(8,128)S(1)} %get-tuple-element.95, f32[16,24,511]{2,1,0:T(8,128)S(1)} %get-tuple-element.94, f32[16,23,512]{2,1,0:T(8,128)S(1)} %get-tuple-element.93, f32[16,23,512]{2,1,0:T(8,128)S(1)} %get-tuple-element.92, ...), kind=kLoop, calls=%fused_computation.222 | loop fusion | flops 5111808 | bytes 13300760 | tf_op jit(solution)/shard_map/jit(_where)/select_n | solution.py:144
  215.7 2.4 %slice_multiply_fusion = (f32[16,24,512]{2,1,0:T(8,128)S(1)}, f32[16,24,512]{2,1,0:T(8,128)S(1)}) fusion(f32[16,40,512]{2,1,0:T(8,128)S(1)} %copy-done.30, f32[16,24,512]{2,1,0:T(8,128)S(1)} %fusion.135, f32[16,40,512]{2,1,0:T(8,128)S(1)} %copy-done.15, f32[16,24,511]{2,1,0:T(8,128)S(1)} %get-tuple-element.89, f32[16,42,512]{2,1,0:T(8,128)S(1)} %copy-done.7, ...), kind=kLoop, calls=%fused_computation.230 | loop fusion | flops 5308416 | bytes 14087192 | tf_op jit(solution)/shard_map/mul | solution.py:92
  219.9 2.0 fusion.132
  (411 shorter events, 106.3 us)
Async XLA Ops:
  3.8 11.3 %collective-permute-start = (f32[34,16,128]{2,1,0:T(8,128)}, f32[34,16,128]{2,1,0:T(8,128)S(1)}, u32[]{:S(2)}, u32[]{:S(2)}) collective-permute-start(f32[34,16,128]{2,1,0:T(8,128)} %pad_maximum_fusion.6), channel_id=1, source_target_pairs={{0,24},{8,0},{16,8},{24,16},{1,25},{9,1},{17,9},{25,17},{2,26},{10... | collective-permute-start | bytes 835592 | tf_op jit(solution)/shard_map/ppermute | solution.py:44
  7.7 14.3 %collective-permute-start.1 = (f32[34,16,128]{2,1,0:T(8,128)}, f32[34,16,128]{2,1,0:T(8,128)S(1)}, u32[]{:S(2)}, u32[]{:S(2)}) collective-permute-start(f32[34,16,128]{2,1,0:T(8,128)} %pad_maximum_fusion.6), channel_id=1, source_target_pairs={{0,16},{8,24},{16,0},{24,8},{1,17},{9,25},{17,1},{25,9},{2,18},{10... | collective-permute-start | bytes 835592 | tf_op jit(solution)/shard_map/ppermute | solution.py:44
  8.2 13.8 %collective-permute-start.2 = (f32[34,16,128]{2,1,0:T(8,128)}, f32[34,16,128]{2,1,0:T(8,128)S(1)}, u32[]{:S(2)}, u32[]{:S(2)}) collective-permute-start(f32[34,16,128]{2,1,0:T(8,128)} %pad_maximum_fusion.6), channel_id=1, source_target_pairs={{0,8},{8,16},{16,24},{24,0},{1,9},{9,17},{17,25},{25,1},{2,10},{10... | collective-permute-start | bytes 835592 | tf_op jit(solution)/shard_map/ppermute | solution.py:44
  24.3 25.1 %collective-permute-start.4 = (f32[34,13,512]{2,0,1:T(8,128)S(1)}, f32[34,13,512]{2,0,1:T(8,128)S(1)}, u32[]{:S(2)}, u32[]{:S(2)}) collective-permute-start(f32[34,13,512]{2,0,1:T(8,128)S(1)} %copy.29), channel_id=1, source_target_pairs={{2,0},{4,2},{6,4},{3,1},{5,3},{7,5},{10,8},{12,10},{14,12},{11,9},... | collective-permute-start | bytes 2715656 | tf_op jit(solution)/shard_map/ppermute | solution.py:36
  27.1 25.3 %collective-permute-start.3 = (f32[34,13,512]{2,0,1:T(8,128)}, f32[34,13,512]{2,0,1:T(8,128)S(1)}, u32[]{:S(2)}, u32[]{:S(2)}) collective-permute-start(f32[34,13,512]{2,0,1:T(8,128)} %copy.28), channel_id=1, source_target_pairs={{0,2},{2,4},{4,6},{1,3},{3,5},{5,7},{8,10},{10,12},{12,14},{9,11},... | collective-permute-start | bytes 2715656 | tf_op jit(solution)/shard_map/ppermute | solution.py:35
  59.3 4.1 %collective-permute-start.5 = (f32[1,42,512]{2,1,0:T(8,128)S(1)}, f32[1,42,512]{2,1,0:T(8,128)S(1)}, u32[]{:S(2)}, u32[]{:S(2)}) collective-permute-start(f32[1,42,512]{2,1,0:T(8,128)S(1)} %maximum_select_fusion), channel_id=1, source_target_pairs={{0,1},{1,0},{2,3},{3,2},{4,5},{5,4},{6,7},{7,6},{8,9},{9,8},{10,11... | collective-permute-start | bytes 258056 | tf_op jit(solution)/shard_map/ppermute | solution.py:25
  88.1 9.6 %collective-permute-start.6 = (f32[1,40,512]{2,1,0:T(8,128)S(1)}, f32[1,40,512]{2,1,0:T(8,128)S(1)}, u32[]{:S(2)}, u32[]{:S(2)}) collective-permute-start(f32[1,40,512]{2,1,0:T(8,128)S(1)} %slice_select_fusion.3), channel_id=1, source_target_pairs={{0,1},{1,0},{2,3},{3,2},{4,5},{5,4},{6,7},{7,6},{8,9},{9,8},{10,11... | collective-permute-start | bytes 245768 | tf_op jit(solution)/shard_map/ppermute | solution.py:25
  102.4 1.3 collective-permute-start.7
  108.5 1.3 collective-permute-start.8
  114.6 1.3 collective-permute-start.9
  126.4 1.6 collective-permute-start.10
  128.9 1.3 collective-permute-start.11
  131.0 1.3 collective-permute-start.12
  133.1 1.3 collective-permute-start.15
  137.4 11.5 %collective-permute-start.16 = (f32[128,4,128]{2,0,1:T(8,128)}, f32[128,4,128]{2,0,1:T(8,128)}, u32[]{:S(2)}, u32[]{:S(2)}) collective-permute-start(f32[128,4,128]{2,0,1:T(8,128)} %fusion.66), channel_id=1, source_target_pairs={{0,6},{2,0},{4,2},{6,4},{1,7},{3,1},{5,3},{7,5},{8,14},{10,8},{12,... | collective-permute-start | bytes 786440 | tf_op jit(solution)/shard_map/ppermute | solution.py:44
  141.9 23.1 %collective-permute-start.17 = (f32[128,4,128]{2,0,1:T(8,128)}, f32[128,4,128]{2,0,1:T(8,128)}, u32[]{:S(2)}, u32[]{:S(2)}) collective-permute-start(f32[128,4,128]{2,0,1:T(8,128)} %fusion.66), channel_id=1, source_target_pairs={{0,4},{2,6},{4,0},{6,2},{1,5},{3,7},{5,1},{7,3},{8,12},{10,14},{12... | collective-permute-start | bytes 786440 | tf_op jit(solution)/shard_map/ppermute | solution.py:44
  141.9 24.0 %collective-permute-start.18 = (f32[128,4,128]{2,0,1:T(8,128)}, f32[128,4,128]{2,0,1:T(8,128)S(1)}, u32[]{:S(2)}, u32[]{:S(2)}) collective-permute-start(f32[128,4,128]{2,0,1:T(8,128)} %fusion.66), channel_id=1, source_target_pairs={{0,2},{2,4},{4,6},{6,0},{1,3},{3,5},{5,7},{7,1},{8,10},{10,12},{12... | collective-permute-start | bytes 786440 | tf_op jit(solution)/shard_map/ppermute | solution.py:44
  171.5 13.3 %collective-permute-start.19 = (f32[128,16,128]{2,0,1:T(8,128)}, f32[128,16,128]{2,0,1:T(8,128)}, u32[]{:S(2)}, u32[]{:S(2)}) collective-permute-start(f32[128,16,128]{2,0,1:T(8,128)} %get-tuple-element.77), channel_id=1, source_target_pairs={{0,1},{1,0},{2,3},{3,2},{4,5},{5,4},{6,7},{7,6},{8,9},{9,8},{10,11... | collective-permute-start | bytes 3145736 | tf_op jit(solution)/shard_map/ppermute | solution.py:44
  172.9 10.6 %collective-permute-start.14 = (f32[32,6,256]{2,1,0:T(8,128)S(1)}, f32[32,6,256]{2,1,0:T(8,128)S(1)}, u32[]{:S(2)}, u32[]{:S(2)}) collective-permute-start(f32[32,6,256]{2,1,0:T(8,128)S(1)} %get-tuple-element.204), channel_id=1, source_target_pairs={{2,0},{4,2},{6,4},{3,1},{5,3},{7,5},{10,8},{12,10},{14,12},{11,9},... | collective-permute-start | bytes 589832 | tf_op jit(solution)/shard_map/ppermute | solution.py:36
  174.2 10.5 %collective-permute-start.13 = (f32[32,6,256]{2,1,0:T(8,128)S(1)}, f32[32,6,256]{2,1,0:T(8,128)S(1)}, u32[]{:S(2)}, u32[]{:S(2)}) collective-permute-start(f32[32,6,256]{2,1,0:T(8,128)S(1)} %get-tuple-element.203), channel_id=1, source_target_pairs={{0,2},{2,4},{4,6},{1,3},{3,5},{5,7},{8,10},{10,12},{12,14},{9,11},... | collective-permute-start | bytes 589832 | tf_op jit(solution)/shard_map/ppermute | solution.py:35
  203.8 1.3 collective-permute-start.24
  210.2 1.3 collective-permute-start.25
  214.4 1.3 collective-permute-start.26
  218.6 1.3 collective-permute-start.27
  (55 other events, 768.0 us)
